TPU v7x, 256 devices: a whole 4x4x8 slice. The times are simulated.
256 devices in a mesh: dp: 4 (over z_hi), ctx: 16 (over y, z_lo, core), tp: 4 (over x).
Axes of the slice: x: 4, y: 4, z: 8 (z_hi: 4, z_lo: 2; z = z_hi * 2 + z_lo), core: 2. Of those that a mesh axis runs over, the one named last changes fastest.
Arguments:
- queries: bfloat16 [12288, 4096], P(('dp', 'ctx'), 'tp'), parts along dimension 0, may hold values from -40 to 40
- keys: bfloat16 [12288, 512], P(('dp', 'ctx'), 'tp'), parts along dimension 0, may hold values from -4 to 4
- values: bfloat16 [12288, 512], P(('dp', 'ctx'), 'tp'), parts along dimension 0, may hold values from -6 to 6
- grad_out: bfloat16 [12288, 4096], P(('dp', 'ctx'), 'tp'), parts along dimension 0, may hold values from -6 to 6
- segments: int32 [12288], P(('dp', 'ctx')), parts along dimension 0, may hold values from 0 to 5, never falling along the last dimension, each value on 1 to 2304 neighbouring positions
- sinks: float32 [64], P('tp'), may hold values from -1 to 5
Outputs:
- grad_queries: bfloat16 [12288, 4096], P(('dp', 'ctx'), 'tp'), parts along dimension 0
- keys_gradient: bfloat16 [12288, 512], P(('dp', 'ctx'), 'tp'), parts along dimension 0
- values_gradient: bfloat16 [12288, 512], P(('dp', 'ctx'), 'tp'), parts along dimension 0
- grad_sinks: float32 [256], P(('dp', 'tp')), parts along dimension 0
There are 4 independent parts, one for each index of `dp`. A program takes and returns all parts, laid end to end along the dimension named above; an argument that names none is the same for every part. Nothing has to cross between parts.
All inputs are finite; a program needn't handle non-finite values.
Results may differ from a plain program's by a relative error of at most 0.012.
The roundings to bfloat16 on the way count: a program that leaves them out, or rounds other values in their place, can miss the bound.
Values may be sent and summed in bfloat16 or wider, within the bound.
A program may use at most 64 MiB of HBM per device.

v0:
```python
import jax
import jax.numpy as jnp
from jax import lax
from jax.sharding import PartitionSpec as P

HEAD_SIZE = 64


NEG_FILL = -1e30


def side_by_side(arrays, axis, dim, along):
    both = jnp.concatenate(arrays, axis=along)
    filled, at, gathered = (lax.all_gather(both, axis, axis=dim, tiled=True), 0, [])
    for a in arrays:
        gathered.append(lax.slice_in_dim(filled, at, at + a.shape[along], axis=along))
        at += a.shape[along]
    return tuple(gathered)


def laid_out(pieces, dim):
    shape = list(pieces.shape[1:])
    shape[dim] *= pieces.shape[0]
    return jnp.moveaxis(pieces, 0, dim).reshape(shape)


def from_everyone(x, axis):
    copies = jnp.broadcast_to(x, (lax.axis_size(axis), *x.shape))
    return lax.all_to_all(copies, axis, split_axis=0, concat_axis=0, tiled=True)


def collect(x, axis, dim):
    return laid_out(from_everyone(x, axis), dim)


def of_everyone(x, axis):
    everything = from_everyone(x, axis)
    return jnp.sum(everything, axis=0)


def in_blocks(x, dim, peers):
    before, after = (x.shape[:dim], x.shape[dim + 1 :])
    return jnp.moveaxis(x.reshape(*before, peers, -1, *after), dim, 0)


def sum_at_owner(x, axis, dim):
    pieces = in_blocks(x, dim, lax.axis_size(axis))
    arrived = lax.all_to_all(pieces, axis, split_axis=0, concat_axis=0, tiled=True)
    return arrived.sum(axis=0)


def in_one_piece(arrays, axis, dim, along):
    ends, at = ([], 0)
    for a in arrays[:-1]:
        at += a.shape[along]
        ends.append(at)
    both = jnp.concatenate(arrays, axis=along)
    return tuple(jnp.split(sum_at_owner(both, axis, dim), ends, axis=along))


def head_major(block, kv_heads):
    length = block.shape[0]
    query_group = block.shape[1] // (kv_heads * HEAD_SIZE)
    return (
        block.reshape(length, kv_heads, query_group, HEAD_SIZE)
        .transpose(1, 2, 0, 3)
        .reshape(kv_heads, query_group * length, HEAD_SIZE)
    )


def row_major(stacked, length):
    kv_heads = stacked.shape[0]
    query_group = stacked.shape[1] // length
    return (
        stacked.reshape(kv_heads, query_group, length, HEAD_SIZE)
        .transpose(2, 0, 1, 3)
        .reshape(length, kv_heads * query_group * HEAD_SIZE)
    )


def add_rows(buffer, term, start):
    length = term.shape[1]
    flat = term.transpose(1, 0, 2).reshape(length, term.shape[0] * HEAD_SIZE)
    before = lax.dynamic_slice_in_dim(buffer, start, length, 0)
    return lax.dynamic_update_slice_in_dim(buffer, before + flat, start, 0)


def on_device(queries, keys, values, grad_out, segments, sinks):
    length = queries.shape[0]
    kv_heads = keys.shape[1] // HEAD_SIZE
    query_group = queries.shape[1] // keys.shape[1]
    scale = HEAD_SIZE ** (-0.5)
    place = lax.axis_index("ctx")
    key_all, value_all = side_by_side((keys, values), "ctx", 0, 1)
    seg_all = collect(segments, "ctx", 0)
    total_sum = key_all.shape[0]
    key_heads = key_all.reshape(total_sum, kv_heads, HEAD_SIZE).transpose(1, 0, 2)
    value_heads = value_all.reshape(total_sum, kv_heads, HEAD_SIZE).transpose(1, 0, 2)

    def tile_scores(query_heads, query_seg, query_first, tile):
        start = tile * length
        key_block = lax.dynamic_slice_in_dim(key_heads, start, length, 1)
        value_block = lax.dynamic_slice_in_dim(value_heads, start, length, 1)
        raw = (
            lax.dot_general(
                query_heads,
                key_block,
                (((2,), (2,)), ((0,), (0,))),
                preferred_element_type=jnp.float32,
            )
            * scale
        )
        key_seg = lax.dynamic_slice_in_dim(seg_all, start, length, 0)
        query_pos = query_first + lax.iota(jnp.int32, length)
        key_pos = start + lax.iota(jnp.int32, length)
        allowed = (key_pos[None, :] <= query_pos[:, None]) & (
            key_seg[None, :] == query_seg[:, None]
        )
        allowed = jnp.tile(allowed, (query_group, 1))[None]
        return (raw, allowed, key_block, value_block)

    home_q = head_major(queries, kv_heads)
    home_grad = head_major(grad_out, kv_heads)
    first = place * length
    row_shape = (kv_heads, query_group * length)
    sink_rows = jnp.broadcast_to(
        sinks.reshape(kv_heads, query_group, 1), (kv_heads, query_group, length)
    ).reshape(row_shape)

    def stat_step(tile, carry):
        top, mass = carry
        raw, allowed, key_block, value_block = tile_scores(home_q, segments, first, tile)
        masked = jnp.where(allowed, raw, NEG_FILL)
        new_top = jnp.maximum(top, jnp.max(masked, axis=-1))
        weight = jnp.where(allowed, jnp.exp(raw - new_top[..., None]), 0.0)
        mass = mass * jnp.exp(top - new_top) + jnp.sum(weight, axis=-1)
        return (new_top, mass)

    top, mass = lax.fori_loop(
        0, place + 1, stat_step, (sink_rows, jnp.ones(row_shape, jnp.float32))
    )
    lse_rows = top + jnp.log(mass)

    def out_step(tile, total_out):
        raw, allowed, key_block, value_block = tile_scores(home_q, segments, first, tile)
        prob_half = jnp.where(allowed, jnp.exp(raw - lse_rows[..., None]), 0.0).astype(jnp.bfloat16)
        return total_out + lax.dot_general(
            prob_half, value_block, (((2,), (1,)), ((0,), (0,))), preferred_element_type=jnp.float32
        )

    out = lax.fori_loop(0, place + 1, out_step, jnp.zeros(home_q.shape, jnp.float32))
    delta_rows = jnp.sum(home_grad.astype(jnp.float32) * out, axis=-1)
    stats = jnp.stack([lse_rows, delta_rows])
    sink_term = -jnp.sum(
        (jnp.exp(sink_rows - lse_rows) * delta_rows).reshape(kv_heads, query_group, length), axis=-1
    ).reshape(kv_heads * query_group)
    grad_sinks = of_everyone(sink_term, "ctx")
    buffers = (
        jnp.zeros((total_sum, kv_heads * HEAD_SIZE), jnp.float32),
        jnp.zeros((total_sum, kv_heads * HEAD_SIZE), jnp.float32),
    )
    home_low = 0
    stat_lse = stats[0]
    stat_delta = stats[1]

    def step(tile, carry):
        grad_acc, key_buf, value_buf = carry
        raw, allowed, key_block, value_block = tile_scores(home_q, segments, first, tile)
        prob = jnp.where(allowed, jnp.exp(raw - stat_lse[..., None]), 0.0)
        prob_half = prob.astype(jnp.bfloat16)
        dprob = lax.dot_general(
            home_grad, value_block, (((2,), (2,)), ((0,), (0,))), preferred_element_type=jnp.float32
        )
        dscore = (prob * (dprob - stat_delta[..., None])).astype(jnp.bfloat16)
        grad_acc = (
            grad_acc
            + lax.dot_general(
                dscore, key_block, (((2,), (1,)), ((0,), (0,))), preferred_element_type=jnp.float32
            )
            * scale
        )
        key_term = (
            lax.dot_general(
                dscore, home_q, (((1,), (1,)), ((0,), (0,))), preferred_element_type=jnp.float32
            )
            * scale
        )
        value_term = lax.dot_general(
            prob_half, home_grad, (((1,), (1,)), ((0,), (0,))), preferred_element_type=jnp.float32
        )
        key_buf = add_rows(key_buf, key_term, tile * length)
        value_buf = add_rows(value_buf, value_term, tile * length)
        return (grad_acc, key_buf, value_buf)

    start_acc = jnp.zeros(home_q.shape, jnp.float32)
    grad_home, key_buf, value_buf = lax.fori_loop(
        home_low, place + 1, step, (start_acc, buffers[0], buffers[1])
    )
    grad_rows = row_major(grad_home, length)
    key_own, value_own = in_one_piece((key_buf, value_buf), "ctx", 0, 1)
    return (
        grad_rows.astype(jnp.bfloat16),
        key_own.astype(jnp.bfloat16),
        value_own.astype(jnp.bfloat16),
        grad_sinks,
    )


def solution(mesh):
    placed = (
        P(("dp", "ctx"), "tp"),
        P(("dp", "ctx"), "tp"),
        P(("dp", "ctx"), "tp"),
        P(("dp", "ctx"), "tp"),
        P(("dp", "ctx")),
        P("tp"),
    )
    return jax.shard_map(
        on_device,
        mesh=mesh,
        in_specs=placed,
        out_specs=(
            P(("dp", "ctx"), "tp"),
            P(("dp", "ctx"), "tp"),
            P(("dp", "ctx"), "tp"),
            P(("dp", "tp")),
        ),
        check_vma=False,
    )
```

profile of v0, /device:TPU:1, one launch (start us, length us, event | category | flops | bytes accessed | tf_op | source)
XLA Modules:
  0.0 379.1 jit_solution(15506464785045918451)
XLA Ops:
  7.2 1.5 pad_maximum_fusion.1
  8.8 1.3 broadcast_in_dim.64
  10.1 7.3 %all-to-all-start = ((s32[16,1,192]{2,1,0:T(1,128)}), s32[16,1,192]{2,1,0:T(1,128)S(1)}, u32[]{:S(2)}, u32[]{:S(2)}) async-start(s32[16,1,192]{2,1,0:T(1,128)} %broadcast_in_dim.64), calls=%async_computation | async-start | bytes 32768 | tf_op jit(solution)/shard_map/all_to_all | solution.py:29
  17.4 0.7 broadcast_in_dim.65
  18.3 1.2 copy.48
  19.5 0.3 copy.49
  19.8 0.4 reshape.266
  20.2 0.2 copy.51
  20.4 0.3 copy.52
  20.8 0.4 reshape.270
  21.2 2.0 all-to-all-done
  23.3 27.1 %all-gather.2.cloned.1.call-done = bf16[3072,256]{1,0:T(8,128)(2,1)} async-done(((bf16[192,256]{1,0:T(8,128)(2,1)}), bf16[3072,256]{1,0:T(8,128)(2,1)}) %all-gather.2.cloned.1.call-update) | async-done | bytes 1572880 | tf_op jit(solution)/shard_map/all_gather | solution.py:14
  50.4 1.5 fusion.35
  51.9 1.2 copy.50
  53.1 1.2 copy.47
  54.3 6.8 %while.36 = (s32[]{:T(128)}, f32[2,1536]{1,0:T(2,128)S(1)}, f32[2,1536]{1,0:T(2,128)S(1)}, s32[]{:T(128)}, s32[]{:T(128)}, /*index=5*/s32[3072]{0:T(1024)S(1)}, ...) while((s32[]{:T(128)}, f32[2,1536]{1,0:T(2,128)S(1)}, ...), condition=%wide.region_3.4_spmd, body=%wide.region_0.3_spmd.sunk | while | flops 79153544 | bytes 6891707 | solution.py:139
  54.5 0.2 tile.33
  54.7 0.7 tile.34
  55.5 1.6 select_reduce_fusion.4
  57.1 0.5 select_reduce_fusion.5
  57.9 0.2 tile.33
  58.1 0.7 tile.34
  58.8 1.6 select_reduce_fusion.4
  60.5 0.5 select_reduce_fusion.5
  61.2 6.5 %while.37 = (s32[]{:T(128)}, f32[2,1536,64]{1,2,0:T(8,128)S(1)}, s32[]{:T(128)}, s32[]{:T(128)}, s32[3072]{0:T(1024)S(1)}, /*index=5*/s32[192]{0:T(256)S(1)}, bf...) while((s32[]{:T(128)}, f32[2,1536,64]{1,2,0:T(8,128)S(1)}, ...), condition=%wide.region_5.6_spmd, body=%wide.region_4.5_spmd.sunk | while | flops 153661824 | bytes 3370175 | solution.py:151
  61.4 0.2 tile.35
  61.6 0.7 tile.36
  62.4 2.0 convolution_add_fusion.2
  64.7 0.2 tile.35
  64.8 0.7 tile.36
  65.6 2.0 convolution_add_fusion.2
  68.1 0.6 broadcast_in_dim.68
  68.7 96.1 %all-to-all-start.2 = ((f32[16,1,16]{2,1,0:T(1,128)}), f32[16,1,16]{2,1,0:T(1,128)S(1)}, u32[]{:S(2)}, u32[]{:S(2)}) async-start(f32[16,1,16]{2,1,0:T(1,128)} %broadcast_in_dim.68), calls=%async_computation.2 | async-start | bytes 16384 | tf_op jit(solution)/shard_map/all_to_all | solution.py:29
  164.8 1.3 broadcast.194.clone2
  166.1 1.3 broadcast.194.clone
  167.4 19.3 %while.38 = (s32[]{:T(128)}, f32[2,1536,64]{1,2,0:T(8,128)S(1)}, f32[3072,128]{1,0:T(8,128)}, f32[3072,128]{1,0:T(8,128)}, s32[]{:T(128)}, /*index=5*/s32[]{:T(1...) while((s32[]{:T(128)}, f32[2,1536,64]{1,2,0:T(8,128)S(1)}, ...), condition=%wide.region_8.9_spmd, body=%wide.region_7.8_spmd.sunk | while | flops 382194048 | bytes 17602808 | solution.py:196
  167.6 0.9 constant_dynamic-slice_fusion.4
  168.6 0.9 constant_dynamic-slice_fusion.5
  169.6 0.2 tile.37
  169.8 0.7 tile.38
  170.5 1.7 fusion.77
  172.3 0.5 fusion.80
  172.8 1.5 fusion.78
  174.4 0.5 convolution_multiply_fusion.6
  174.9 1.3 fusion.79
  176.3 0.7 constant_dynamic-update-slice_fusion.3
  177.2 0.9 constant_dynamic-slice_fusion.4
  178.2 0.9 constant_dynamic-slice_fusion.5
  179.3 0.2 tile.37
  179.4 0.7 tile.38
  180.2 1.8 fusion.77
  182.0 0.5 fusion.80
  182.5 1.5 fusion.78
  184.1 0.5 convolution_multiply_fusion.6
  184.6 1.3 fusion.79
  186.0 0.7 constant_dynamic-update-slice_fusion.3
  186.7 3.7 pad_maximum_fusion
  190.4 140.6 %all-to-all-start.1 = ((f32[16,192,256]{2,1,0:T(8,128)}), f32[16,192,256]{2,1,0:T(8,128)}, u32[]{:S(2)}, u32[]{:S(2)}) async-start(f32[16,192,256]{2,1,0:T(8,128)} %bitcast.95), calls=%async_computation.1 | async-start | bytes 6291456 | tf_op jit(solution)/shard_map/all_to_all | solution.py:48
  331.1 0.4 convert_element_type.28
  331.6 0.9 copy.57
  332.5 0.5 reduce_sum.48
  333.1 36.4 %all-to-all-done.1 = f32[16,192,256]{2,1,0:T(8,128)} async-done(((f32[16,192,256]{2,1,0:T(8,128)}), f32[16,192,256]{2,1,0:T(8,128)}, u32[]{:S(2)}, u32[]{:S(2)}) %all-to-all-start.1) | async-done | bytes 3145760 | tf_op jit(solution)/shard_map/all_to_all | solution.py:48
  369.5 2.1 reduce_sum.46
  371.6 0.6 fusion.36
  (67 shorter events, 3.2 us)
Async XLA Ops:
  7.2 13.1 %copy-start.3 = (bf16[192,1024]{1,0:T(8,128)(2,1)S(1)}, bf16[192,1024]{1,0:T(8,128)(2,1)}, u32[]{:S(2)}) copy-start(bf16[192,1024]{1,0:T(8,128)(2,1)} %param.15) | copy-start | bytes 1179652
  7.2 43.2 %all-gather.2.cloned.1.call-start = ((), (), s32[]{:S(2)}) async-start(), calls=%async_computation.3 | async-start | bytes 1671168 | tf_op jit(solution)/shard_map/all_gather | solution.py:14
  10.1 13.1 %all-to-all-start = ((s32[16,1,192]{2,1,0:T(1,128)}), s32[16,1,192]{2,1,0:T(1,128)S(1)}, u32[]{:S(2)}, u32[]{:S(2)}) async-start(s32[16,1,192]{2,1,0:T(1,128)} %broadcast_in_dim.64), calls=%async_computation | async-start | bytes 32768 | tf_op jit(solution)/shard_map/all_to_all | solution.py:29
  18.3 2.5 copy-start
  51.9 2.4 copy-start.2
  51.9 2.4 copy-start.4
  61.2 6.6 %copy-start.1 = (f32[2,1536]{1,0:T(2,128)S(1)}, f32[2,1536]{1,0:T(2,128)}, u32[]{:S(2)}) copy-start(f32[2,1536]{1,0:T(2,128)} %copy-done) | copy-start | bytes 36868
  68.7 121.8 %all-to-all-start.2 = ((f32[16,1,16]{2,1,0:T(1,128)}), f32[16,1,16]{2,1,0:T(1,128)S(1)}, u32[]{:S(2)}, u32[]{:S(2)}) async-start(f32[16,1,16]{2,1,0:T(1,128)} %broadcast_in_dim.68), calls=%async_computation.2 | async-start | bytes 16384 | tf_op jit(solution)/shard_map/all_to_all | solution.py:29
  190.4 179.0 %all-to-all-start.1 = ((f32[16,192,256]{2,1,0:T(8,128)}), f32[16,192,256]{2,1,0:T(8,128)}, u32[]{:S(2)}, u32[]{:S(2)}) async-start(f32[16,192,256]{2,1,0:T(8,128)} %bitcast.95), calls=%async_computation.1 | async-start | bytes 6291456 | tf_op jit(solution)/shard_map/all_to_all | solution.py:48
Sparse Core Ops, SparseCore 0:
  10.4 39.9 all-gather.1
where the time goes:
time: 383 us; the launch traced here: 379 us
  starting transfers between devices  244 us (64%)
  waiting for transfers between devices  65.5 us (17%)
  local copies, waits for them, and re-layouts  26.3 us (7%)
  matrix products  18.5 us (5%)
  between operations  14.2 us (4%)
  other arithmetic  10.1 us (3%)
    all_to_all x1, starting transfers between devices, sum_at_owner(): lax.all_to_all(pieces, axis, split_axis=0, concat_axis=0, tiled=True)  141 us
    all_to_all x2, starting transfers between devices, from_everyone(): return lax.all_to_all(copies, axis, split_axis=0, concat_axis=0, tiled=True)  103 us
    all_to_all x1, waiting for transfers between devices, sum_at_owner(): lax.all_to_all(pieces, axis, split_axis=0, concat_axis=0, tiled=True)  36.4 us
    all_gather x1, waiting for transfers between devices, side_by_side(): lax.all_gather(both, axis, axis=dim, tiled=True)  27.1 us
  transfers between devices with their start and end apart: 4, of which 3 were waited for; matrix products, arithmetic and copies ran while one was open for 9% of the time, Pallas kernels for 0%

commit v1 on v0

v1 whole, which is shorter than its diff:
```python
import functools

import jax
import jax.numpy as jnp
from jax import lax
from jax.experimental import pallas as pl
from jax.experimental.pallas import tpu as pltpu
from jax.sharding import PartitionSpec as P

D = 64
PEERS = 16
ROWS = 192
HALF = 96
DOCS = 6
TILE = 128
LANES = 2 * TILE
CHUNK = 256
LOG2E = 1.4426950408889634
FILL = -1e30
f32 = jnp.float32
bf16 = jnp.bfloat16


def spot(i):
    return i // 4, lax.rem(i // 2, 2), lax.rem(i, 2)


def remote(src, dst, send, recv, to):
    return pltpu.make_async_remote_copy(
        src_ref=src,
        dst_ref=dst,
        send_sem=send,
        recv_sem=recv,
        device_id={"ctx": to},
        device_id_type=pl.DeviceIdType.MESH,
    )


def greet(me):
    barrier = pltpu.get_barrier_semaphore()

    def hello(i, c):
        to = lax.rem(me + i, PEERS)
        pl.semaphore_signal(
            barrier, inc=1, device_id={"ctx": to}, device_id_type=pl.DeviceIdType.MESH
        )
        return c

    lax.fori_loop(1, PEERS, hello, 0)
    pl.semaphore_wait(barrier, PEERS - 1)


def scatter_kernel(
    q_ref, g_ref, k_ref, v_ref, seg_ref,
    qo_ref, go_ref, kvo_ref, cnt_ref,
    kvbuf, cntbuf, cntall,
    qs, qr, gs, gr, ks, kr, fs, cs, cr, ls,
):
    me = lax.axis_index("ctx")
    y, z, c = spot(me)
    mate = me + 1 - 2 * c

    for h in range(2):
        kvbuf[h] = jnp.concatenate(
            [k_ref[:, h * D : (h + 1) * D], v_ref[:, h * D : (h + 1) * D]], axis=1
        )
    lane = lax.broadcasted_iota(jnp.int32, (1, 128), 1)
    row = jnp.zeros((1, 128), f32)
    for d in range(1, DOCS):
        below = jnp.sum(jnp.where(seg_ref[...] < d, 1.0, 0.0), axis=1, keepdims=True)
        row = jnp.where(lane == d, below, row)
    cntbuf[...] = row
    cntall[me] = row

    greet(me)

    def q_copy(to, frm):
        ty, tz, tc = spot(to)
        rows = pl.ds(pl.multiple_of(tc * HALF, 32), HALF)
        cols = pl.ds(pl.multiple_of(tz * 512 + ty * 128, 128), 128)
        land = pl.ds(pl.multiple_of(frm * HALF, 32), HALF)
        return (
            (q_ref.at[rows, cols], qo_ref.at[land], qs.at[to], qr.at[frm]),
            (g_ref.at[rows, cols], go_ref.at[land], gs.at[to], gr.at[frm]),
        )

    def kv_at(i):
        return kvo_ref.at[pl.ds(pl.multiple_of(i * ROWS, 64), ROWS)]

    (a, b) = q_copy(me, me)
    own_q = pltpu.make_async_copy(a[0], a[1], ls.at[0])
    own_g = pltpu.make_async_copy(b[0], b[1], ls.at[1])
    own_kv = pltpu.make_async_copy(kvbuf.at[z], kv_at(me), ls.at[2])
    own_q.start()
    own_g.start()
    own_kv.start()

    def kv_send(i, carry):
        to = lax.rem(me + 2 * i, PEERS)
        remote(kvbuf.at[spot(to)[1]], kv_at(me), ks.at[to], kr.at[me], to).start()
        return carry

    lax.fori_loop(1, 8, kv_send, 0)
    remote(kvbuf.at[z], kv_at(me), ks.at[mate], kr.at[me], mate).start()

    def cnt_send(i, carry):
        to = lax.rem(me + i, PEERS)
        remote(cntbuf, cntall.at[me], cs.at[to], cr.at[me], to).start()
        return carry

    lax.fori_loop(1, PEERS, cnt_send, 0)

    def q_send(i, carry):
        to = lax.rem(me + i, PEERS)
        for s in q_copy(to, me):
            remote(*s, to).start()
        return carry

    lax.fori_loop(1, PEERS, q_send, 0)

    def kv_pass(i, carry):
        frm = lax.rem(me + PEERS - 2 * i, PEERS)
        remote(kvbuf.at[0], kv_at(frm), ks.at[frm], kr.at[frm], frm).wait_recv()
        remote(kv_at(frm), kv_at(frm), fs.at[frm], kr.at[frm], mate).start()
        return carry

    lax.fori_loop(1, 8, kv_pass, 0)

    def kv_get(i, carry):
        frm = lax.rem(mate + 2 * i, PEERS)
        remote(kvbuf.at[0], kv_at(frm), ks.at[frm], kr.at[frm], frm).wait_recv()
        return carry

    lax.fori_loop(0, 8, kv_get, 0)

    def kv_sent(i, carry):
        to = lax.rem(me + 2 * i, PEERS)
        remote(kvbuf.at[0], kv_at(me), ks.at[to], kr.at[me], to).wait_send()
        remote(kv_at(to), kv_at(to), fs.at[to], kr.at[to], mate).wait_send()
        return carry

    lax.fori_loop(1, 8, kv_sent, 0)
    remote(kvbuf.at[0], kv_at(me), ks.at[mate], kr.at[me], mate).wait_send()

    def rest(i, carry):
        o = lax.rem(me + i, PEERS)
        for s in q_copy(o, o):
            cp = remote(*s, o)
            cp.wait_send()
            cp.wait_recv()
        cp = remote(cntbuf, cntall.at[o], cs.at[o], cr.at[o], o)
        cp.wait_send()
        cp.wait_recv()
        return carry

    lax.fori_loop(1, PEERS, rest, 0)
    own_q.wait()
    own_g.wait()
    own_kv.wait()
    total = cntall[0]
    for i in range(1, PEERS):
        total = total + cntall[i]
    cnt_ref[...] = total


def scatter(q, g, k, v, seg):
    any_ = pl.BlockSpec(memory_space=pl.ANY)
    vmem = pl.BlockSpec(memory_space=pltpu.VMEM)
    sem = pltpu.SemaphoreType.DMA
    total = PEERS * ROWS
    return pl.pallas_call(
        scatter_kernel,
        name="scatter",
        out_shape=(
            jax.ShapeDtypeStruct((total // 2, 128), bf16),
            jax.ShapeDtypeStruct((total // 2, 128), bf16),
            jax.ShapeDtypeStruct((total, 128), bf16),
            jax.ShapeDtypeStruct((1, 128), f32),
        ),
        in_specs=[any_, any_, vmem, vmem, vmem],
        out_specs=(any_, any_, any_, vmem),
        scratch_shapes=[
            pltpu.VMEM((2, ROWS, 128), bf16),
            pltpu.VMEM((1, 128), f32),
            pltpu.VMEM((PEERS, 1, 128), f32),
        ]
        + [sem((PEERS,))] * 9
        + [sem((3,))],
        compiler_params=pltpu.CompilerParams(collective_id=0, has_side_effects=True),
    )(q, g, k, v, seg)


def local_kernel(
    cnt_ref, sink_ref, q_ref, g_ref, kv_ref,
    dq_ref, dkv_ref, gs_ref,
    kt_ref, acc_ref, s_ref, dp_ref, gacc_ref,
):
    me = lax.axis_index("ctx")
    y, z, c = spot(me)
    total = kv_ref.shape[0]
    head = 8 * z + 2 * y
    begins = [cnt_ref[0, d].astype(jnp.int32) for d in range(1, DOCS)]

    acc_ref[...] = jnp.zeros_like(acc_ref)
    gacc_ref[...] = jnp.zeros_like(gacc_ref)

    def turn(j, carry):
        at = pl.multiple_of(j * CHUNK, CHUNK)
        both = kv_ref[pl.ds(at, CHUNK), :].astype(f32).T
        kt_ref[j] = both[:D].astype(bf16)
        return carry

    lax.fori_loop(0, total // CHUNK, turn, 0)

    lane = lax.broadcasted_iota(jnp.int32, (1, LANES), 1)
    sink = jnp.where(lane < TILE, sink_ref[head], sink_ref[head + 1])
    key_iota = lax.broadcasted_iota(jnp.int32, (CHUNK, LANES), 0)
    nt = (((1,), (1,)), ((), ()))

    def fold(x, op):
        return op(x.reshape(CHUNK // 8, 8, LANES), axis=0)

    def tile(t, carry):
        n0 = pl.multiple_of(t * TILE, TILE)
        s0 = n0 // HALF
        n = n0 + (lane & (TILE - 1))
        pos = n + HALF * (s0 + c) + jnp.where(n >= (s0 + 1) * HALF, HALF, 0)
        start = jnp.zeros_like(pos)
        p_first = n0 + HALF * (s0 + c)
        p_last = n0 + TILE - 1 + HALF * (s0 + 1 + c)
        first = 0
        for b in begins:
            start = jnp.where(pos >= b, b, start)
            first = jnp.where(p_first >= b, b, first)
        lo = first // CHUNK
        hi = p_last // CHUNK + 1

        qt = q_ref[pl.ds(n0, TILE), :]
        gt = g_ref[pl.ds(n0, TILE), :]
        qt = (qt.astype(f32) * 0.125).astype(bf16)
        none = jnp.zeros((TILE, D), bf16)
        wq = jnp.concatenate(
            [
                jnp.concatenate([qt[:, :D], none], axis=1),
                jnp.concatenate([qt[:, D:], none], axis=1),
            ],
            axis=0,
        )
        wg = jnp.concatenate(
            [
                jnp.concatenate([none, gt[:, :D]], axis=1),
                jnp.concatenate([none, gt[:, D:]], axis=1),
            ],
            axis=0,
        )
        w = jnp.concatenate([wq, wg], axis=0)

        def scores(j, top):
            kv = kv_ref[pl.ds(pl.multiple_of(j * CHUNK, CHUNK), CHUNK), :]
            at = pl.ds(pl.multiple_of((j - lo) * CHUNK, CHUNK), CHUNK)
            s = lax.dot_general(kv, wq, nt, preferred_element_type=f32)
            key = key_iota + j * CHUNK
            s = jnp.where((key >= start) & (key <= pos), s, FILL)
            s_ref[at, :] = s
            dp_ref[at, :] = lax.dot_general(kv, wg, nt, preferred_element_type=f32)
            return jnp.maximum(top, fold(s, jnp.max))

        top = lax.fori_loop(lo, hi, scores, jnp.full((8, LANES), FILL, f32))
        top = jnp.maximum(jnp.max(top, axis=0, keepdims=True), sink)

        def weights(j, mass):
            at = pl.ds(pl.multiple_of((j - lo) * CHUNK, CHUNK), CHUNK)
            e = jnp.exp2((s_ref[at, :] - top) * LOG2E)
            s_ref[at, :] = e
            return mass + fold(e, jnp.sum)

        mass = lax.fori_loop(lo, hi, weights, jnp.zeros((8, LANES), f32))
        sink_e = jnp.exp2((sink - top) * LOG2E)
        mass = jnp.sum(mass, axis=0, keepdims=True) + sink_e
        inv = 1.0 / mass

        def deltas(j, delta):
            at = pl.ds(pl.multiple_of((j - lo) * CHUNK, CHUNK), CHUNK)
            half = (s_ref[at, :] * inv).astype(bf16).astype(f32)
            return delta + fold(half * dp_ref[at, :], jnp.sum)

        delta = lax.fori_loop(lo, hi, deltas, jnp.zeros((8, LANES), f32))
        delta = jnp.sum(delta, axis=0, keepdims=True)
        gacc_ref[...] += sink_e * inv * delta

        def grads(j, dqt):
            at = pl.ds(pl.multiple_of((j - lo) * CHUNK, CHUNK), CHUNK)
            key = pl.ds(pl.multiple_of(j * CHUNK, CHUNK), CHUNK)
            prob = s_ref[at, :] * inv
            ds = (prob * (dp_ref[at, :] - delta)).astype(bf16)
            x = jnp.concatenate([ds, prob.astype(bf16)], axis=1)
            acc_ref[key, :] += jnp.dot(x, w, preferred_element_type=f32)
            return dqt + jnp.dot(kt_ref[j], ds, preferred_element_type=f32)

        dqt = lax.fori_loop(lo, hi, grads, jnp.zeros((D, LANES), f32))
        dq = (dqt * 0.125).T
        dq_ref[pl.ds(n0, TILE), :] = jnp.concatenate([dq[:TILE], dq[TILE:]], axis=1).astype(bf16)
        return carry

    lax.fori_loop(0, q_ref.shape[0] // TILE, tile, 0)
    dkv_ref[...] = acc_ref[...].astype(bf16)
    g = gacc_ref[...]
    ga = -jnp.sum(g[:, :TILE], axis=1, keepdims=True)
    gb = -jnp.sum(g[:, TILE:], axis=1, keepdims=True)
    l = lax.broadcasted_iota(jnp.int32, (1, 128), 1)
    gs_ref[...] = jnp.where(l == head, ga, jnp.where(l == head + 1, gb, 0.0))


def local(cnt, sinks, q, g, kv):
    vmem = pl.BlockSpec(memory_space=pltpu.VMEM)
    smem = pl.BlockSpec(memory_space=pltpu.SMEM)
    total = kv.shape[0]
    return pl.pallas_call(
        local_kernel,
        name="local",
        out_shape=(
            jax.ShapeDtypeStruct(q.shape, bf16),
            jax.ShapeDtypeStruct(kv.shape, bf16),
            jax.ShapeDtypeStruct((1, 128), f32),
        ),
        in_specs=[smem, smem, vmem, vmem, vmem],
        out_specs=(vmem, vmem, vmem),
        scratch_shapes=[
            pltpu.VMEM((total // CHUNK, D, CHUNK), bf16),
            pltpu.VMEM((total, 128), f32),
            pltpu.VMEM((total, LANES), f32),
            pltpu.VMEM((total, LANES), f32),
            pltpu.VMEM((1, LANES), f32),
        ],
        compiler_params=pltpu.CompilerParams(vmem_limit_bytes=40 * 1024 * 1024),
    )(cnt, sinks, q, g, kv)


def gather_kernel(
    dq_ref, dkv_ref, gs_ref,
    dqo_ref, dk_ref, dv_ref, gso_ref,
    own, mine, sums, land, gall,
    qs, qr, ms, mr, ss, sr, cs, cr, ls,
):
    me = lax.axis_index("ctx")
    y, z, c = spot(me)
    mate = me + 1 - 2 * c
    gall[me] = gs_ref[...]
    pull = pltpu.make_async_copy(dkv_ref.at[:, c], own, ls.at[0])
    pull.start()

    greet(me)

    def mate_send(i, carry):
        b = lax.rem(2 * y + z + i, 8)
        remote(dkv_ref.at[b, 1 - c], mine.at[b], ms.at[b], mr.at[b], mate).start()
        return carry

    lax.fori_loop(0, 8, mate_send, 0)

    def q_copy(to, frm):
        fy, fz, fc = spot(frm)
        rows = pl.ds(pl.multiple_of(fc * HALF, 32), HALF)
        cols = pl.ds(pl.multiple_of(fz * 512 + fy * 128, 128), 128)
        take = pl.ds(pl.multiple_of(to * HALF, 32), HALF)
        return dq_ref.at[take], dqo_ref.at[rows, cols], qs.at[to], qr.at[frm]

    a = q_copy(me, me)
    own_q = pltpu.make_async_copy(a[0], a[1], ls.at[1])
    own_q.start()

    def g_send(i, carry):
        to = lax.rem(me + i, PEERS)
        remote(gs_ref, gall.at[me], cs.at[to], cr.at[me], to).start()
        return carry

    lax.fori_loop(1, PEERS, g_send, 0)

    def q_send(i, carry):
        to = lax.rem(me + i, PEERS)
        remote(*q_copy(to, me), to).start()
        return carry

    lax.fori_loop(1, PEERS, q_send, 0)
    pull.wait()

    def chip_sum(b):
        remote(dkv_ref.at[b, c], mine.at[b], ms.at[b], mr.at[b], mate).wait_recv()
        return (own[b].astype(f32) + mine[b].astype(f32)).astype(bf16)

    def sum_send(i, carry):
        b = lax.rem(2 * y + z + i, 8)
        sums[b] = chip_sum(b)
        to = 2 * b + c
        remote(sums.at[b], land.at[2 * y + z], ss.at[b], sr.at[2 * y + z], to).start()
        return carry

    lax.fori_loop(1, 8, sum_send, 0)
    land[2 * y + z] = chip_sum(2 * y + z)

    def sum_get(i, carry):
        b = lax.rem(2 * y + z + i, 8)
        cp = remote(sums.at[b], land.at[b], ss.at[b], sr.at[b], 2 * b + c)
        cp.wait_send()
        cp.wait_recv()
        return carry

    lax.fori_loop(1, 8, sum_get, 0)
    heads = []
    for h in range(2):
        heads.append(
            (land[h].astype(f32) + land[2 + h].astype(f32))
            + (land[4 + h].astype(f32) + land[6 + h].astype(f32))
        )
    dk_ref[...] = jnp.concatenate([heads[0][:, :D], heads[1][:, :D]], axis=1).astype(bf16)
    dv_ref[...] = jnp.concatenate([heads[0][:, D:], heads[1][:, D:]], axis=1).astype(bf16)

    def rest(i, carry):
        o = lax.rem(me + i, PEERS)
        cp = remote(*q_copy(o, o), o)
        cp.wait_send()
        cp.wait_recv()
        cp = remote(gs_ref, gall.at[o], cs.at[o], cr.at[o], o)
        cp.wait_send()
        cp.wait_recv()
        return carry

    lax.fori_loop(1, PEERS, rest, 0)

    def mate_sent(b, carry):
        remote(dkv_ref.at[b, 1 - c], mine.at[b], ms.at[b], mr.at[b], mate).wait_send()
        return carry

    lax.fori_loop(0, 8, mate_sent, 0)
    own_q.wait()
    total = gall[0]
    for i in range(1, PEERS):
        total = total + gall[i]
    gso_ref[...] = total


def gather(dq, dkv, gs):
    any_ = pl.BlockSpec(memory_space=pl.ANY)
    vmem = pl.BlockSpec(memory_space=pltpu.VMEM)
    sem = pltpu.SemaphoreType.DMA
    blocks = pltpu.VMEM((8, ROWS, 128), bf16)
    return pl.pallas_call(
        gather_kernel,
        name="gather",
        out_shape=(
            jax.ShapeDtypeStruct((ROWS, 1024), bf16),
            jax.ShapeDtypeStruct((ROWS, 128), bf16),
            jax.ShapeDtypeStruct((ROWS, 128), bf16),
            jax.ShapeDtypeStruct((1, 128), f32),
        ),
        in_specs=[any_, any_, vmem],
        out_specs=(any_, vmem, vmem, vmem),
        scratch_shapes=[blocks, blocks, blocks, blocks, pltpu.VMEM((PEERS, 1, 128), f32)]
        + [sem((PEERS,))] * 2
        + [sem((8,))] * 4
        + [sem((PEERS,))] * 2
        + [sem((2,))],
        compiler_params=pltpu.CompilerParams(collective_id=1, has_side_effects=True),
    )(dq, dkv.reshape(8, 2, ROWS, 128), gs)


def on_device(queries, keys, values, grad_out, segments, sinks):
    q, g, kv, cnt = scatter(queries, grad_out, keys, values, segments.reshape(1, ROWS))
    dq, dkv, gs = local(cnt, sinks, q, g, kv)
    grad_q, dk, dv, grad_sinks = gather(dq, dkv, gs)
    return grad_q, dk, dv, grad_sinks.reshape(128)[: sinks.shape[0]]


def solution(mesh):
    rows = P(("dp", "ctx"), "tp")
    return jax.shard_map(
        on_device,
        mesh=mesh,
        in_specs=(rows, rows, rows, rows, P(("dp", "ctx")), P("tp")),
        out_specs=(rows, rows, rows, P(("dp", "tp"))),
        check_vma=False,
    )
```

time: 383 us -> 92.9 us (0.24)
  the two profiles are of different devices: /device:TPU:1 before, /device:TPU:135 now
where the time goes in v1:
time: 92.9 us; the launch traced here: 92.5 us
  Pallas kernels  81.5 us (88%)
  local copies, waits for them, and re-layouts  10.3 us (11%)
    pallas_call x1, Pallas kernels, local(): pl.pallas_call(local_kernel, name='local', out_shape=(jax.ShapeDtypeStruc...  41.4 us
    pallas_call x1, Pallas kernels, scatter(): pl.pallas_call(scatter_kernel, name='scatter', out_shape=(jax.ShapeDtypeS...  22.1 us
    pallas_call x1, Pallas kernels, gather(): pl.pallas_call(gather_kernel, name='gather', out_shape=(jax.ShapeDtypeStr...  17.9 us
    unnamed x25, local copies, waits for them, and re-layouts  9.82 us

profile of v1, /device:TPU:135, one launch (start us, length us, event | category | flops | bytes accessed | tf_op | source)
XLA Modules:
  0.0 92.5 jit_solution(782179665378102434)
XLA Ops:
  0.6 22.1 %scatter.1 = (bf16[1536,128]{1,0:T(8,128)(2,1)}, bf16[1536,128]{1,0:T(8,128)(2,1)}, bf16[3072,128]{1,0:T(8,128)(2,1)}, f32[1,128]{1,0:T(1,128)}) custom-call(bf16[192,1024]{1,0:T(8,128)(2,1)} %q_ref.1, bf16[192,1024]{1,0:T(8,128)(2,1)} %g_ref.1, bf16[192,128]{1,0:T(8,128)(2,1)} %k_ref.1, bf16[192,128]{1,0:T(8,128)(2,1)} %v_ref.1, s32[1,192]{1,0:T(1,128)} %bitcast.5), custom_call_target="tpu_custom_call" | custom-call | tf_op jit(solution)/shard_map/scatter/pallas_call | solution.py:171
  22.8 0.0 copy-start.5
  22.8 0.0 copy-start.7
  22.8 0.6 copy-done.5
  23.4 0.0 copy-done.7
  23.5 0.0 copy-start.1
  23.5 1.1 %copy-done.1 = bf16[3072,128]{1,0:T(8,128)(2,1)S(1)} copy-done((bf16[3072,128]{1,0:T(8,128)(2,1)S(1)}, bf16[3072,128]{1,0:T(8,128)(2,1)}, u32[]{:S(2)}) %copy-start.1) | copy-done | bytes 786456
  24.6 0.0 copy-start.3
  24.6 1.0 %copy-done.3 = bf16[1536,128]{1,0:T(8,128)(2,1)S(1)} copy-done((bf16[1536,128]{1,0:T(8,128)(2,1)S(1)}, bf16[1536,128]{1,0:T(8,128)(2,1)}, u32[]{:S(2)}) %copy-start.3) | copy-done | bytes 393240
  25.6 0.0 copy-start.4
  25.6 1.0 %copy-done.4 = bf16[1536,128]{1,0:T(8,128)(2,1)S(1)} copy-done((bf16[1536,128]{1,0:T(8,128)(2,1)S(1)}, bf16[1536,128]{1,0:T(8,128)(2,1)}, u32[]{:S(2)}) %copy-start.4) | copy-done | bytes 393240
  26.6 41.4 %local.1 = (bf16[1536,128]{1,0:T(8,128)(2,1)S(1)}, bf16[3072,128]{1,0:T(8,128)(2,1)S(1)}, f32[1,128]{1,0:T(1,128)S(1)}) custom-call(f32[1,128]{1,0:T(1,128)S(1)} %copy-done.7, f32[16]{0:T(128)S(1)} %copy-done.5, bf16[1536,128]{1,0:T(8,128)(2,1)S(1)} %copy-done.3, bf16[1536,128]{1,0:T(8,128)(2,1)S(1)} %copy-done.4, bf16[3072,128]{1,0:T(8,128)(2,1)S(1)} %copy-done.1), custom_call_target="tpu_custom_call" | custom-call | tf_op jit(solution)/shard_map/local/pallas_call | solution.py:318
  68.0 0.0 copy-start
  68.1 0.9 copy-done
  68.9 0.0 copy-start.2
  69.0 0.7 copy-done.2
  69.7 0.0 copy-start.6
  69.7 0.5 copy-done.6
  70.2 17.9 %gather.1 = (bf16[192,1024]{1,0:T(8,128)(2,1)}, bf16[192,128]{1,0:T(8,128)(2,1)}, bf16[192,128]{1,0:T(8,128)(2,1)}, f32[1,128]{1,0:T(1,128)}) custom-call(bf16[1536,128]{1,0:T(8,128)(2,1)} %copy-done.2, bf16[8,2,192,128]{3,2,1,0:T(8,128)(2,1)} %bitcast.4, f32[1,128]{1,0:T(1,128)} %copy-done.6), custom_call_target="tpu_custom_call" | custom-call | tf_op jit(solution)/shard_map/gather/pallas_call | solution.py:447
  88.2 0.0 copy-start.10
  88.2 0.7 copy-done.10
  88.8 0.5 slice_bitcast_fusion
  89.3 0.0 copy-start.9
  89.3 1.8 %copy.13 = bf16[192,1024]{1,0:T(8,128)(2,1)} copy(bf16[192,1024]{1,0:T(8,128)(2,1)} %get-tuple-element.30) | data formatting | bytes 786432
  91.1 0.0 copy-done.9
  91.1 0.0 copy-start.8
  91.1 0.6 copy.14
  91.7 0.2 copy-done.8
  91.9 0.6 copy.15
Async XLA Ops:
  22.8 0.7 copy-start.5
  22.8 0.7 copy-start.7
  23.5 1.1 %copy-start.1 = (bf16[3072,128]{1,0:T(8,128)(2,1)S(1)}, bf16[3072,128]{1,0:T(8,128)(2,1)}, u32[]{:S(2)}) copy-start(bf16[3072,128]{1,0:T(8,128)(2,1)} %get-tuple-element.18.kv_ref) | copy-start | bytes 2359300
  24.6 1.0 %copy-start.3 = (bf16[1536,128]{1,0:T(8,128)(2,1)S(1)}, bf16[1536,128]{1,0:T(8,128)(2,1)}, u32[]{:S(2)}) copy-start(bf16[1536,128]{1,0:T(8,128)(2,1)} %get-tuple-element.16.q_ref) | copy-start | bytes 1179652
  25.6 1.0 %copy-start.4 = (bf16[1536,128]{1,0:T(8,128)(2,1)S(1)}, bf16[1536,128]{1,0:T(8,128)(2,1)}, u32[]{:S(2)}) copy-start(bf16[1536,128]{1,0:T(8,128)(2,1)} %get-tuple-element.17.g_ref) | copy-start | bytes 1179652
  68.0 0.9 copy-start
  68.9 0.7 copy-start.2
  69.7 0.5 copy-start.6
  88.2 0.7 copy-start.10
  89.3 1.8 %copy-start.9 = (bf16[192,128]{1,0:T(8,128)(2,1)S(1)}, bf16[192,128]{1,0:T(8,128)(2,1)}, u32[]{:S(2)}) copy-start(bf16[192,128]{1,0:T(8,128)(2,1)} %get-tuple-element.31) | copy-start | bytes 147460
  91.1 0.8 copy-start.8

commit v2 on v1

v2 whole, which is shorter than its diff:
```python
import functools

import jax
import jax.numpy as jnp
from jax import lax
from jax.experimental import pallas as pl
from jax.experimental.pallas import tpu as pltpu
from jax.sharding import PartitionSpec as P

D = 64
PEERS = 16
ROWS = 192
DOCS = 6
TILE = 128
LANES = 2 * TILE
UNIT = 128
SUB = 2
PAD = 4
SIZES = (2, 4, 8, 12, 16, 20)
FAR = 1 << 20
LOG2E = 1.4426950408889634
FILL = -1e30
f32 = jnp.float32
bf16 = jnp.bfloat16


def spot(i):
    return i // 4, lax.rem(i // 2, 2), lax.rem(i, 2)


def is_full(block, core):
    tile = (3 * block + lax.rem(block, 2)) // 2
    return 1 - lax.rem(tile + core, 2)


def piece(block, full):
    odd = lax.rem(block, 2)
    first = odd if full else 2 - 2 * odd
    g = 3 * block + first
    return 64 * first, (g // 4) * TILE + lax.rem(g, 2) * 64


def remote(src, dst, send, recv, to):
    return pltpu.make_async_remote_copy(
        src_ref=src,
        dst_ref=dst,
        send_sem=send,
        recv_sem=recv,
        device_id={"ctx": to},
        device_id_type=pl.DeviceIdType.MESH,
    )


def greet(me):
    barrier = pltpu.get_barrier_semaphore()

    def hello(i, c):
        to = lax.rem(me + i, PEERS)
        pl.semaphore_signal(
            barrier, inc=1, device_id={"ctx": to}, device_id_type=pl.DeviceIdType.MESH
        )
        return c

    lax.fori_loop(1, PEERS, hello, 0)
    pl.semaphore_wait(barrier, PEERS - 1)


def scatter_kernel(
    q_ref, g_ref, k_ref, v_ref, seg_ref,
    qo_ref, go_ref, kvo_ref, cnt_ref,
    kvbuf, cntbuf, cntall,
    qs, qr, gs, gr, ks, kr, fs, cs, cr, ls,
):
    me = lax.axis_index("ctx")
    y, z, c = spot(me)
    mate = me + 1 - 2 * c

    for h in range(2):
        kvbuf[h] = jnp.concatenate(
            [k_ref[:, h * D : (h + 1) * D], v_ref[:, h * D : (h + 1) * D]], axis=1
        )
    lane = lax.broadcasted_iota(jnp.int32, (1, 128), 1)
    row = jnp.zeros((1, 128), f32)
    for d in range(1, DOCS):
        below = jnp.sum(jnp.where(seg_ref[...] < d, 1.0, 0.0), axis=1, keepdims=True)
        row = jnp.where(lane == d, below, row)
    cntbuf[...] = row
    cntall[me] = row

    greet(me)

    def q_copies(to, frm, start=None):
        ty, tz, tc = spot(to)
        cols = pl.ds(pl.multiple_of(tz * 512 + ty * 128, 128), 128)

        def each(full, size):
            @pl.when(is_full(frm, tc) == full)
            def _():
                src, dst = piece(frm, full)
                rows = pl.ds(pl.multiple_of(src, 64), size)
                land = pl.ds(pl.multiple_of(dst, 64), size)
                start(q_ref.at[rows, cols], qo_ref.at[land], qs.at[to], qr.at[frm])
                start(g_ref.at[rows, cols], go_ref.at[land], gs.at[to], gr.at[frm])

        each(1, TILE)
        each(0, TILE // 2)

    def kv_at(i):
        return kvo_ref.at[pl.ds(pl.multiple_of(i * ROWS, 64), ROWS)]

    q_copies(me, me, lambda src, dst, x, sem: pltpu.make_async_copy(src, dst, sem).start())
    own_kv = pltpu.make_async_copy(kvbuf.at[z], kv_at(me), ls.at[0])
    own_kv.start()

    def kv_send(i, carry):
        to = lax.rem(me + 2 * i, PEERS)
        remote(kvbuf.at[spot(to)[1]], kv_at(me), ks.at[to], kr.at[me], to).start()
        return carry

    lax.fori_loop(1, 8, kv_send, 0)
    remote(kvbuf.at[z], kv_at(me), ks.at[mate], kr.at[me], mate).start()

    def cnt_send(i, carry):
        to = lax.rem(me + i, PEERS)
        remote(cntbuf, cntall.at[me], cs.at[to], cr.at[me], to).start()
        return carry

    lax.fori_loop(1, PEERS, cnt_send, 0)

    def q_send(i, carry):
        to = lax.rem(me + i, PEERS)
        q_copies(to, me, lambda *p: remote(*p, to).start())
        return carry

    lax.fori_loop(1, PEERS, q_send, 0)

    def kv_pass(i, carry):
        frm = lax.rem(me + PEERS - 2 * i, PEERS)
        remote(kvbuf.at[0], kv_at(frm), ks.at[frm], kr.at[frm], frm).wait_recv()
        remote(kv_at(frm), kv_at(frm), fs.at[frm], kr.at[frm], mate).start()
        return carry

    lax.fori_loop(1, 8, kv_pass, 0)

    def kv_get(i, carry):
        frm = lax.rem(mate + 2 * i, PEERS)
        remote(kvbuf.at[0], kv_at(frm), ks.at[frm], kr.at[frm], frm).wait_recv()
        return carry

    lax.fori_loop(0, 8, kv_get, 0)

    def kv_sent(i, carry):
        to = lax.rem(me + 2 * i, PEERS)
        remote(kvbuf.at[0], kv_at(me), ks.at[to], kr.at[me], to).wait_send()
        remote(kv_at(to), kv_at(to), fs.at[to], kr.at[to], mate).wait_send()
        return carry

    lax.fori_loop(1, 8, kv_sent, 0)
    remote(kvbuf.at[0], kv_at(me), ks.at[mate], kr.at[me], mate).wait_send()

    def rest(i, carry):
        o = lax.rem(me + i, PEERS)
        q_copies(o, me, lambda *p: remote(*p, o).wait_send())
        q_copies(me, o, lambda src, dst, x, sem: remote(src, dst, x, sem, o).wait_recv())
        cp = remote(cntbuf, cntall.at[o], cs.at[o], cr.at[o], o)
        cp.wait_send()
        cp.wait_recv()
        return carry

    lax.fori_loop(1, PEERS, rest, 0)
    q_copies(me, me, lambda src, dst, x, sem: pltpu.make_async_copy(src, dst, sem).wait())
    own_kv.wait()
    total = cntall[0]
    for i in range(1, PEERS):
        total = total + cntall[i]
    cnt_ref[...] = total


def scatter(q, g, k, v, seg):
    any_ = pl.BlockSpec(memory_space=pl.ANY)
    vmem = pl.BlockSpec(memory_space=pltpu.VMEM)
    sem = pltpu.SemaphoreType.DMA
    total = PEERS * ROWS
    return pl.pallas_call(
        scatter_kernel,
        name="scatter",
        out_shape=(
            jax.ShapeDtypeStruct((total // 2, 128), bf16),
            jax.ShapeDtypeStruct((total // 2, 128), bf16),
            jax.ShapeDtypeStruct((total, 128), bf16),
            jax.ShapeDtypeStruct((1, 128), f32),
        ),
        in_specs=[any_, any_, vmem, vmem, vmem],
        out_specs=(vmem, vmem, vmem, vmem),
        scratch_shapes=[
            pltpu.VMEM((2, ROWS, 128), bf16),
            pltpu.VMEM((1, 128), f32),
            pltpu.VMEM((PEERS, 1, 128), f32),
        ]
        + [sem((PEERS,))] * 9
        + [sem((1,))],
        compiler_params=pltpu.CompilerParams(collective_id=0, has_side_effects=True),
    )(q, g, k, v, seg)


def local_kernel(
    cnt_hbm, sink_hbm, q_ref, g_ref, kv_ref,
    dq_ref, dkv_ref, gs_ref,
    cnt_ref, sink_ref, kvf_ref, kt_ref, acc_ref, s_ref, dp_ref, gacc_ref, w_ref, doc_ref, sem,
):
    me = lax.axis_index("ctx")
    y, z, c = spot(me)
    total = kv_ref.shape[0]
    head = 8 * z + 2 * y
    get_cnt = pltpu.make_async_copy(cnt_hbm, cnt_ref, sem.at[0])
    get_sink = pltpu.make_async_copy(sink_hbm, sink_ref, sem.at[1])
    get_cnt.start()
    get_sink.start()
    acc_ref[...] = jnp.zeros_like(acc_ref)
    gacc_ref[...] = jnp.zeros_like(gacc_ref)
    get_cnt.wait()
    get_sink.wait()

    begins = [cnt_ref[0, d].astype(jnp.int32) for d in range(1, DOCS)]
    doc = lax.broadcasted_iota(jnp.int32, (1, 128), 1)
    starts = jnp.zeros((1, 128), jnp.int32)
    ends = jnp.full((1, 128), FAR, jnp.int32)
    for d in range(1, DOCS):
        starts = jnp.where(doc == d, begins[d - 1], starts)
        if d < DOCS - 1:
            ends = jnp.where(doc == d, begins[d], ends)
    q_starts = jnp.where((doc >= 1) & (doc < DOCS), starts, FAR)

    pad = PAD * UNIT
    kvf_ref[:pad, :128] = jnp.zeros((pad, 128), bf16)
    ahead = lax.broadcasted_iota(jnp.int32, (pad, 128), 1) == 0
    kvf_ref[:pad, 128:] = jnp.where(ahead, 1.0, 0.0).astype(bf16)
    kt_ref[:PAD] = jnp.zeros((PAD, D, UNIT), bf16)
    row_256 = lax.broadcasted_iota(jnp.int32, (256, 128), 0)

    def fill(j, carry):
        kv = kv_ref[pl.ds(pl.multiple_of(j * 256, 256), 256), :]
        at = pl.ds(pl.multiple_of(j * 256 + pad, 256), 256)
        kvf_ref[at, :128] = kv
        kvf_ref[at, 128:] = jnp.where(row_256 + j * 256 < starts, 1.0, 0.0).astype(bf16)
        kt = kv.astype(f32).T[:D].astype(bf16)
        kt_ref[2 * j + PAD] = kt[:, :UNIT]
        kt_ref[2 * j + 1 + PAD] = kt[:, UNIT:]
        return carry

    lax.fori_loop(0, total // 256, fill, 0)

    lane = lax.broadcasted_iota(jnp.int32, (1, LANES), 1)
    sink = jnp.where(lane < TILE, sink_ref[head], sink_ref[head + 1])
    row = lax.broadcasted_iota(jnp.int32, (TILE, 128), 0)
    below = lax.broadcasted_iota(jnp.int32, (UNIT, LANES), 0) <= (lane & (TILE - 1))
    nt = (((1,), (1,)), ((), ()))

    def fold(x, op):
        return op(x.reshape(x.shape[0] // 8, 8, LANES), axis=0)

    def tile(t, carry):
        n0 = pl.multiple_of(t * TILE, TILE)
        place = 2 * t + c
        p0 = place * TILE
        first = 0
        for b in begins:
            first = jnp.where(p0 >= b, b, first)
        units = place - first // UNIT + 1
        qt = (q_ref[pl.ds(n0, TILE), :].astype(f32) * 0.125).astype(bf16)
        gt = g_ref[pl.ds(n0, TILE), :]
        none = jnp.zeros((TILE, D), bf16)
        w_ref[:TILE] = jnp.concatenate([qt[:, :D], none], axis=1)
        w_ref[TILE : 2 * TILE] = jnp.concatenate([qt[:, D:], none], axis=1)
        w_ref[2 * TILE : 3 * TILE] = jnp.concatenate([none, gt[:, :D]], axis=1)
        w_ref[3 * TILE :] = jnp.concatenate([none, gt[:, D:]], axis=1)
        inside = (row + p0 >= q_starts) & (row + p0 < ends)
        doc_ref[...] = jnp.where((doc == 0) | inside, FILL, 0.0).astype(bf16)

        def run(size):
            wg = w_ref[2 * TILE :]
            docs = jnp.concatenate([doc_ref[...]] * 2, axis=0)
            wq = jnp.concatenate([w_ref[: 2 * TILE], docs], axis=1)
            u0 = place + 1 - size + PAD

            def rows(i):
                return pl.ds(pl.multiple_of((u0 + i) * UNIT, UNIT), SUB * UNIT)

            subs = list(range(0, size, SUB))[::-1]
            top = sink
            mass = jnp.zeros((8, LANES), f32)
            tops = {}
            for i in subs:
                kv = kvf_ref[rows(i), :]
                at = slice(i * UNIT, (i + SUB) * UNIT)
                s = lax.dot_general(kv, wq, nt, preferred_element_type=f32)
                dp_ref[at, :] = lax.dot_general(kv[:, :128], wg, nt, preferred_element_type=f32)
                if i + SUB == size:
                    s = jnp.concatenate(
                        [s[:-UNIT], jnp.where(below, s[-UNIT:], FILL)], axis=0
                    )
                new = jnp.maximum(top, jnp.max(fold(s, jnp.max), axis=0, keepdims=True))
                e = jnp.exp2((s - new) * LOG2E)
                s_ref[at, :] = e
                mass = mass * jnp.exp2((top - new) * LOG2E) + fold(e, jnp.sum)
                top = tops[i] = new
            sink_e = jnp.exp2((sink - top) * LOG2E)
            inv = 1.0 / (jnp.sum(mass, axis=0, keepdims=True) + sink_e)

            delta = jnp.zeros((8, LANES), f32)
            scale = {}
            for i in subs:
                at = slice(i * UNIT, (i + SUB) * UNIT)
                scale[i] = jnp.exp2((tops[i] - top) * LOG2E) * inv
                half = (s_ref[at, :] * scale[i]).astype(bf16).astype(f32)
                delta = delta + fold(half * dp_ref[at, :], jnp.sum)
            delta = jnp.sum(delta, axis=0, keepdims=True)
            gacc_ref[...] += sink_e * inv * delta

            dqt = jnp.zeros((D, LANES), f32)
            w = w_ref[...]
            for i in subs:
                at = slice(i * UNIT, (i + SUB) * UNIT)
                prob = s_ref[at, :] * scale[i]
                ds = (prob * (dp_ref[at, :] - delta)).astype(bf16)
                x = jnp.concatenate([ds, prob.astype(bf16)], axis=1)
                acc_ref[rows(i), :] += jnp.dot(x, w, preferred_element_type=f32)
                kt = jnp.concatenate([kt_ref[u0 + i + j] for j in range(SUB)], axis=1)
                dqt = dqt + jnp.dot(kt, ds, preferred_element_type=f32)
            dq = (dqt * 0.125).T
            dq = jnp.concatenate([dq[:TILE], dq[TILE:]], axis=1)
            dq_ref[pl.ds(n0, TILE), :] = dq.astype(bf16)

        for over, size in zip((0,) + SIZES[:-1], SIZES):
            pl.when((units > over) & (units <= size))(functools.partial(run, size))
        return carry

    lax.fori_loop(0, q_ref.shape[0] // TILE, tile, 0)
    dkv_ref[...] = acc_ref[pad:, :].astype(bf16)
    g = gacc_ref[...]
    ga = -jnp.sum(g[:, :TILE], axis=1, keepdims=True)
    gb = -jnp.sum(g[:, TILE:], axis=1, keepdims=True)
    gs_ref[...] = jnp.where(doc == head, ga, jnp.where(doc == head + 1, gb, 0.0))


def local(cnt, sinks, q, g, kv):
    any_ = pl.BlockSpec(memory_space=pl.ANY)
    vmem = pl.BlockSpec(memory_space=pltpu.VMEM)
    total = kv.shape[0]
    padded = total + PAD * UNIT
    return pl.pallas_call(
        local_kernel,
        name="local",
        out_shape=(
            jax.ShapeDtypeStruct(q.shape, bf16),
            jax.ShapeDtypeStruct(kv.shape, bf16),
            jax.ShapeDtypeStruct((1, 128), f32),
        ),
        in_specs=[any_, any_, vmem, vmem, vmem],
        out_specs=(vmem, vmem, vmem),
        scratch_shapes=[
            pltpu.SMEM((1, 128), f32),
            pltpu.SMEM((16,), f32),
            pltpu.VMEM((padded, 256), bf16),
            pltpu.VMEM((padded // UNIT, D, UNIT), bf16),
            pltpu.VMEM((padded, 128), f32),
            pltpu.VMEM((SIZES[-1] * UNIT, LANES), f32),
            pltpu.VMEM((SIZES[-1] * UNIT, LANES), f32),
            pltpu.VMEM((1, LANES), f32),
            pltpu.VMEM((4 * TILE, 128), bf16),
            pltpu.VMEM((TILE, 128), bf16),
            pltpu.SemaphoreType.DMA((2,)),
        ],
        compiler_params=pltpu.CompilerParams(vmem_limit_bytes=24 * 1024 * 1024),
    )(cnt, sinks, q, g, kv)


def gather_kernel(
    dq_ref, dkv_ref, gs_ref,
    dqo_ref, land, gall,
    mine, sums,
    qs, qr, ms, mr, ss, sr, cs, cr,
):
    me = lax.axis_index("ctx")
    y, z, c = spot(me)
    mate = me + 1 - 2 * c
    gall[me] = gs_ref[...]

    greet(me)

    def mate_send(i, carry):
        b = lax.rem(2 * y + z + i, 8)
        remote(dkv_ref.at[b, 1 - c], mine.at[b], ms.at[b], mr.at[b], mate).start()
        return carry

    lax.fori_loop(0, 8, mate_send, 0)

    def q_copies(to, frm, start):
        fy, fz, fc = spot(frm)
        cols = pl.ds(pl.multiple_of(fz * 512 + fy * 128, 128), 128)

        def each(full, size):
            @pl.when(is_full(to, fc) == full)
            def _():
                dst, src = piece(to, full)
                take = pl.ds(pl.multiple_of(src, 64), size)
                rows = pl.ds(pl.multiple_of(dst, 64), size)
                start(dq_ref.at[take], dqo_ref.at[rows, cols], qs.at[to], qr.at[frm])

        each(1, TILE)
        each(0, TILE // 2)

    q_copies(me, me, lambda src, dst, x, sem: pltpu.make_async_copy(src, dst, sem).start())

    def g_send(i, carry):
        to = lax.rem(me + i, PEERS)
        remote(gs_ref, gall.at[me], cs.at[to], cr.at[me], to).start()
        return carry

    lax.fori_loop(1, PEERS, g_send, 0)

    def q_send(i, carry):
        to = lax.rem(me + i, PEERS)
        q_copies(to, me, lambda *p: remote(*p, to).start())
        return carry

    lax.fori_loop(1, PEERS, q_send, 0)

    def chip_sum(b):
        remote(dkv_ref.at[b, c], mine.at[b], ms.at[b], mr.at[b], mate).wait_recv()
        return (dkv_ref[b, c].astype(f32) + mine[b].astype(f32)).astype(bf16)

    def sum_send(i, carry):
        b = lax.rem(2 * y + z + i, 8)
        sums[b] = chip_sum(b)
        to = 2 * b + c
        remote(sums.at[b], land.at[2 * y + z], ss.at[b], sr.at[2 * y + z], to).start()
        return carry

    lax.fori_loop(1, 8, sum_send, 0)
    land[2 * y + z] = chip_sum(2 * y + z)

    def sum_get(i, carry):
        b = lax.rem(2 * y + z + i, 8)
        cp = remote(sums.at[b], land.at[b], ss.at[b], sr.at[b], 2 * b + c)
        cp.wait_send()
        cp.wait_recv()
        return carry

    lax.fori_loop(1, 8, sum_get, 0)

    def rest(i, carry):
        o = lax.rem(me + i, PEERS)
        q_copies(o, me, lambda *p: remote(*p, o).wait_send())
        q_copies(me, o, lambda src, dst, x, sem: remote(src, dst, x, sem, o).wait_recv())
        cp = remote(gs_ref, gall.at[o], cs.at[o], cr.at[o], o)
        cp.wait_send()
        cp.wait_recv()
        return carry

    lax.fori_loop(1, PEERS, rest, 0)

    def mate_sent(b, carry):
        remote(dkv_ref.at[b, 1 - c], mine.at[b], ms.at[b], mr.at[b], mate).wait_send()
        return carry

    lax.fori_loop(0, 8, mate_sent, 0)
    q_copies(me, me, lambda src, dst, x, sem: pltpu.make_async_copy(src, dst, sem).wait())


def gather(dq, dkv, gs):
    vmem = pl.BlockSpec(memory_space=pltpu.VMEM)
    sem = pltpu.SemaphoreType.DMA
    blocks = pltpu.VMEM((8, ROWS, 128), bf16)
    return pl.pallas_call(
        gather_kernel,
        name="gather",
        out_shape=(
            jax.ShapeDtypeStruct((ROWS, 1024), bf16),
            jax.ShapeDtypeStruct((8, ROWS, 128), bf16),
            jax.ShapeDtypeStruct((PEERS, 1, 128), f32),
        ),
        in_specs=[vmem, vmem, vmem],
        out_specs=(vmem, vmem, vmem),
        scratch_shapes=[blocks, blocks]
        + [sem((PEERS,))] * 2
        + [sem((8,))] * 4
        + [sem((PEERS,))] * 2,
        compiler_params=pltpu.CompilerParams(collective_id=1, has_side_effects=True),
    )(dq, dkv.reshape(8, 2, ROWS, 128), gs)


def finish_kernel(dq_ref, land, gall, dqo_ref, dk_ref, dv_ref, gso_ref, sem):
    out = pltpu.make_async_copy(dq_ref, dqo_ref, sem)
    out.start()
    heads = []
    for h in range(2):
        heads.append(
            (land[h].astype(f32) + land[2 + h].astype(f32))
            + (land[4 + h].astype(f32) + land[6 + h].astype(f32))
        )
    dk_ref[...] = jnp.concatenate([heads[0][:, :D], heads[1][:, :D]], axis=1).astype(bf16)
    dv_ref[...] = jnp.concatenate([heads[0][:, D:], heads[1][:, D:]], axis=1).astype(bf16)
    total = gall[0]
    for i in range(1, PEERS):
        total = total + gall[i]
    gso_ref[...] = total
    out.wait()


def finish(dq, land, gall):
    vmem = pl.BlockSpec(memory_space=pltpu.VMEM)
    return pl.pallas_call(
        finish_kernel,
        name="finish",
        out_shape=(
            jax.ShapeDtypeStruct((ROWS, 1024), bf16),
            jax.ShapeDtypeStruct((ROWS, 128), bf16),
            jax.ShapeDtypeStruct((ROWS, 128), bf16),
            jax.ShapeDtypeStruct((1, 128), f32),
        ),
        in_specs=[vmem, vmem, vmem],
        out_specs=(pl.BlockSpec(memory_space=pl.ANY), vmem, vmem, vmem),
        scratch_shapes=[pltpu.SemaphoreType.DMA],
    )(dq, land, gall)


def on_device(queries, keys, values, grad_out, segments, sinks):
    q, g, kv, cnt = scatter(queries, grad_out, keys, values, segments.reshape(1, ROWS))
    dq, dkv, gs = local(cnt, sinks, q, g, kv)
    grad_q, dk, dv, grad_sinks = finish(*gather(dq, dkv, gs))
    return grad_q, dk, dv, grad_sinks.reshape(128)[: sinks.shape[0]]


def solution(mesh):
    rows = P(("dp", "ctx"), "tp")
    return jax.shard_map(
        on_device,
        mesh=mesh,
        in_specs=(rows, rows, rows, rows, P(("dp", "ctx")), P("tp")),
        out_specs=(rows, rows, rows, P(("dp", "tp"))),
        check_vma=False,
    )
```

time: 92.9 us -> 74.3 us (0.80)
  the two profiles are of different devices: /device:TPU:135 before, /device:TPU:1 now
where the time goes in v2:
time: 74.3 us; the launch traced here: 74 us
  Pallas kernels  66.2 us (89%)
  local copies, waits for them, and re-layouts  7.06 us (10%)
    pallas_call x1, Pallas kernels, scatter(): pl.pallas_call(scatter_kernel, name='scatter', out_shape=(jax.ShapeDtypeS...  24.6 us
    pallas_call x1, Pallas kernels, local(): pl.pallas_call(local_kernel, name='local', out_shape=(jax.ShapeDtypeStruc...  20.8 us
    pallas_call x1, Pallas kernels, gather(): pl.pallas_call(gather_kernel, name='gather', out_shape=(jax.ShapeDtypeStr...  18.3 us
    unnamed x18, local copies, waits for them, and re-layouts  6.55 us
    pallas_call x1, Pallas kernels, finish(): pl.pallas_call(finish_kernel, name='finish', out_shape=(jax.ShapeDtypeStr...  2.51 us

profile of v2, /device:TPU:1, one launch (start us, length us, event | category | flops | bytes accessed | tf_op | source)
XLA Modules:
  0.0 74.0 jit_solution(839946309435919727)
XLA Ops:
  0.6 24.6 %scatter.1 = (bf16[1536,128]{1,0:T(8,128)(2,1)}, bf16[1536,128]{1,0:T(8,128)(2,1)}, bf16[3072,128]{1,0:T(8,128)(2,1)}, f32[1,128]{1,0:T(1,128)}) custom-call(bf16[192,1024]{1,0:T(8,128)(2,1)} %q_ref.1, bf16[192,1024]{1,0:T(8,128)(2,1)} %g_ref.1, bf16[192,128]{1,0:T(8,128)(2,1)} %k_ref.1, bf16[192,128]{1,0:T(8,128)(2,1)} %v_ref.1, s32[1,192]{1,0:T(1,128)} %bitcast.5), custom_call_target="tpu_custom_call" | custom-call | tf_op jit(solution)/shard_map/scatter/pallas_call | solution.py:184
  25.2 0.0 copy-start.5
  25.2 0.0 copy-start.7
  25.3 0.6 copy-done.5
  25.9 0.0 copy-done.7
  25.9 0.0 copy-start.1
  25.9 1.1 %copy-done.1 = bf16[3072,128]{1,0:T(8,128)(2,1)S(1)} copy-done((bf16[3072,128]{1,0:T(8,128)(2,1)S(1)}, bf16[3072,128]{1,0:T(8,128)(2,1)}, u32[]{:S(2)}) %copy-start.1) | copy-done | bytes 786456
  27.0 0.0 copy-start.3
  27.0 1.0 %copy-done.3 = bf16[1536,128]{1,0:T(8,128)(2,1)S(1)} copy-done((bf16[1536,128]{1,0:T(8,128)(2,1)S(1)}, bf16[1536,128]{1,0:T(8,128)(2,1)}, u32[]{:S(2)}) %copy-start.3) | copy-done | bytes 393240
  28.0 0.0 copy-start.4
  28.0 1.0 %copy-done.4 = bf16[1536,128]{1,0:T(8,128)(2,1)S(1)} copy-done((bf16[1536,128]{1,0:T(8,128)(2,1)S(1)}, bf16[1536,128]{1,0:T(8,128)(2,1)}, u32[]{:S(2)}) %copy-start.4) | copy-done | bytes 393240
  29.0 20.8 %local.1 = (bf16[1536,128]{1,0:T(8,128)(2,1)S(1)}, bf16[3072,128]{1,0:T(8,128)(2,1)S(1)}, f32[1,128]{1,0:T(1,128)S(1)}) custom-call(f32[1,128]{1,0:T(1,128)S(1)} %copy-done.7, f32[16]{0:T(128)S(1)} %copy-done.5, bf16[1536,128]{1,0:T(8,128)(2,1)S(1)} %copy-done.3, bf16[1536,128]{1,0:T(8,128)(2,1)S(1)} %copy-done.4, bf16[3072,128]{1,0:T(8,128)(2,1)S(1)} %copy-done.1), custom_call_target="tpu_custom_call" | custom-call | tf_op jit(solution)/shard_map/local/pallas_call | solution.py:351
  49.9 0.0 copy-start
  49.9 0.9 %copy-done = bf16[3072,128]{1,0:T(8,128)(2,1)} copy-done((bf16[3072,128]{1,0:T(8,128)(2,1)}, bf16[3072,128]{1,0:T(8,128)(2,1)S(1)}, u32[]{:S(2)}) %copy-start) | copy-done | bytes 786456
  50.7 0.0 copy-start.2
  50.7 0.7 %copy-done.2 = bf16[1536,128]{1,0:T(8,128)(2,1)} copy-done((bf16[1536,128]{1,0:T(8,128)(2,1)}, bf16[1536,128]{1,0:T(8,128)(2,1)S(1)}, u32[]{:S(2)}) %copy-start.2) | copy-done | bytes 393240
  51.5 0.0 copy-start.6
  51.5 0.5 copy-done.6
  52.0 18.3 %gather.1 = (bf16[192,1024]{1,0:T(8,128)(2,1)}, bf16[8,192,128]{2,1,0:T(8,128)(2,1)}, f32[16,1,128]{2,1,0:T(1,128)}) custom-call(bf16[1536,128]{1,0:T(8,128)(2,1)} %copy-done.2, bf16[8,2,192,128]{3,2,1,0:T(8,128)(2,1)} %bitcast.4, f32[1,128]{1,0:T(1,128)} %copy-done.6), custom_call_target="tpu_custom_call" | custom-call | tf_op jit(solution)/shard_map/gather/pallas_call | solution.py:475
  70.3 2.5 %finish.1 = (bf16[192,1024]{1,0:T(8,128)(2,1)}, bf16[192,128]{1,0:T(8,128)(2,1)}, bf16[192,128]{1,0:T(8,128)(2,1)}, f32[1,128]{1,0:T(1,128)}) custom-call(bf16[192,1024]{1,0:T(8,128)(2,1)} %get-tuple-element.25.dq_ref, bf16[8,192,128]{2,1,0:T(8,128)(2,1)} %get-tuple-element.26.land, f32[16,1,128]{2,1,0:T(1,128)} %get-tuple-element.27.gall), custom_call_target="tpu_custom_call" | custom-call | tf_op jit(solution)/shard_map/finish/pallas_call | solution.py:513
  72.8 0.0 copy-start.8
  72.8 0.6 copy-done.8
  73.5 0.5 slice_bitcast_fusion
Async XLA Ops:
  25.2 0.7 copy-start.5
  25.2 0.6 copy-start.7
  25.9 1.1 %copy-start.1 = (bf16[3072,128]{1,0:T(8,128)(2,1)S(1)}, bf16[3072,128]{1,0:T(8,128)(2,1)}, u32[]{:S(2)}) copy-start(bf16[3072,128]{1,0:T(8,128)(2,1)} %get-tuple-element.21.kv_ref) | copy-start | bytes 2359300
  27.0 1.0 %copy-start.3 = (bf16[1536,128]{1,0:T(8,128)(2,1)S(1)}, bf16[1536,128]{1,0:T(8,128)(2,1)}, u32[]{:S(2)}) copy-start(bf16[1536,128]{1,0:T(8,128)(2,1)} %get-tuple-element.19.q_ref) | copy-start | bytes 1179652
  28.0 1.0 %copy-start.4 = (bf16[1536,128]{1,0:T(8,128)(2,1)S(1)}, bf16[1536,128]{1,0:T(8,128)(2,1)}, u32[]{:S(2)}) copy-start(bf16[1536,128]{1,0:T(8,128)(2,1)} %get-tuple-element.20.g_ref) | copy-start | bytes 1179652
  49.9 0.9 %copy-start = (bf16[3072,128]{1,0:T(8,128)(2,1)}, bf16[3072,128]{1,0:T(8,128)(2,1)S(1)}, u32[]{:S(2)}) copy-start(bf16[3072,128]{1,0:T(8,128)(2,1)S(1)} %get-tuple-element.23) | copy-start | bytes 2359300
  50.7 0.7 %copy-start.2 = (bf16[1536,128]{1,0:T(8,128)(2,1)}, bf16[1536,128]{1,0:T(8,128)(2,1)S(1)}, u32[]{:S(2)}) copy-start(bf16[1536,128]{1,0:T(8,128)(2,1)S(1)} %get-tuple-element.22.dq_ref) | copy-start | bytes 1179652
  51.5 0.5 copy-start.6
  72.8 0.7 copy-start.8

commit v3 on v2

v3 whole, which is shorter than its diff:
```python
import functools

import jax
import jax.numpy as jnp
from jax import lax
from jax.experimental import pallas as pl
from jax.experimental.pallas import tpu as pltpu
from jax.sharding import PartitionSpec as P

D = 64
PEERS = 16
ROWS = 192
TOTAL = PEERS * ROWS
DOCS = 6
TILE = 128
TILES = TOTAL // TILE // 2
LANES = 2 * TILE
UNIT = 128
SUB = 2
PAD = 4
PADDED = TOTAL + PAD * UNIT
SIZES = (2, 4, 8, 12, 16, 20)
LOG2E = 1.4426950408889634
FILL = -1e30
f32 = jnp.float32
bf16 = jnp.bfloat16


def spot(i):
    return i // 4, lax.rem(i // 2, 2), lax.rem(i, 2)


def is_full(block, core):
    tile = (3 * block + lax.rem(block, 2)) // 2
    return 1 - lax.rem(tile + core, 2)


def piece(block, full):
    odd = lax.rem(block, 2)
    first = odd if full else 2 - 2 * odd
    g = 3 * block + first
    return 64 * first, (g // 4) * TILE + lax.rem(g, 2) * 64


def remote(src, dst, send, recv, to):
    return pltpu.make_async_remote_copy(
        src_ref=src,
        dst_ref=dst,
        send_sem=send,
        recv_sem=recv,
        device_id={"ctx": to},
        device_id_type=pl.DeviceIdType.MESH,
    )


def here(src, dst, _, sem):
    return pltpu.make_async_copy(src, dst, sem)


def greet(me):
    barrier = pltpu.get_barrier_semaphore()

    def hello(i, carry):
        to = lax.rem(me + i, PEERS)
        pl.semaphore_signal(
            barrier, inc=1, device_id={"ctx": to}, device_id_type=pl.DeviceIdType.MESH
        )
        return carry

    lax.fori_loop(1, PEERS, hello, 0)
    pl.semaphore_wait(barrier, PEERS - 1)


def fold(x, op):
    return op(x.reshape(x.shape[0] // 8, 8, LANES), axis=0)


def whole_kernel(
    q_ref, g_ref, k_ref, v_ref, seg_ref, sink_ref,
    dqo_ref, dk_ref, dv_ref, gso_ref,
    kvbuf, cntbuf, cntall, ql, gl, kvl, docl, acc_ref, s_ref, dp_ref, gacc_ref, w_ref, doc_ref,
    dqb, half, mine, sums, land, gbuf, gall,
    ks, kr, fs, cs, cr, qs, qr, gs, gr, ds, dr, es, er, ms, mr, ss, sr, ls,
):
    me = lax.axis_index("ctx")
    y, z, c = spot(me)
    chip = me // 2
    mate = me + 1 - 2 * c
    head = 8 * z + 2 * y
    pad = PAD * UNIT

    for h in range(2):
        kvbuf[h] = jnp.concatenate(
            [k_ref[:, h * D : (h + 1) * D], v_ref[:, h * D : (h + 1) * D]], axis=1
        )
    doc = lax.broadcasted_iota(jnp.int32, (1, 128), 1)
    counts = [jnp.zeros((1, 128), f32), jnp.zeros((1, 128), f32)]
    for d in range(1, DOCS):
        below = jnp.sum(jnp.where(seg_ref[...] < d, 1.0, 0.0), axis=1, keepdims=True)
        counts[0] = jnp.where(doc == d, below, counts[0])
        counts[1] = jnp.where(doc == d - 1, below, counts[1])
    for i in range(2):
        cntbuf[i] = counts[i]
        cntall[me, i] = counts[i]

    greet(me)

    def kv_at(i):
        return kvl.at[pl.ds(pl.multiple_of(i * ROWS + pad, 64), ROWS)]

    def q_copies(to, frm, go):
        ty, tz, tc = spot(to)
        cols = pl.ds(pl.multiple_of(tz * 512 + ty * 128, 128), 128)

        def each(full, size):
            @pl.when(is_full(frm, tc) == full)
            def _():
                src, dst = piece(frm, full)
                rows = pl.ds(pl.multiple_of(src, 64), size)
                at = pl.ds(pl.multiple_of(dst, 64), size)
                go(q_ref.at[rows, cols], ql.at[at], qs.at[to], qr.at[frm])
                go(g_ref.at[rows, cols], gl.at[at], gs.at[to], gr.at[frm])

        each(1, TILE)
        each(0, TILE // 2)

    def kv_send(i, carry):
        to = lax.rem(me + PEERS - 2 * i, PEERS)
        remote(kvbuf.at[spot(to)[1]], kv_at(me), ks.at[to], kr.at[me], to).start()
        return carry

    lax.fori_loop(1, 8, kv_send, 0)
    remote(kvbuf.at[z], kv_at(me), ks.at[mate], kr.at[me], mate).start()
    own_kv = pltpu.make_async_copy(kvbuf.at[z], kv_at(me), ls.at[0])
    own_kv.start()

    def cnt_send(i, carry):
        to = lax.rem(me + i, PEERS)
        remote(cntbuf, cntall.at[me], cs.at[to], cr.at[me], to).start()
        return carry

    lax.fori_loop(1, PEERS, cnt_send, 0)
    q_copies(me, me, lambda *p: here(*p).start())
    q_copies(mate, me, lambda *p: remote(*p, mate).start())

    acc_ref[...] = jnp.zeros_like(acc_ref)
    gacc_ref[...] = jnp.zeros_like(gacc_ref)
    kvl[:pad] = jnp.zeros((pad, 128), bf16)
    w_ref[...] = jnp.zeros_like(w_ref)

    def q_send(i, carry):
        for core in range(2):
            to = lax.rem(2 * chip + PEERS - 2 * i, PEERS) + core
            q_copies(to, me, lambda *p: remote(*p, to).start())
        return carry

    def kv_pass(i, carry):
        frm = lax.rem(me + 2 * i, PEERS)
        remote(kvbuf.at[0], kv_at(frm), ks.at[frm], kr.at[frm], frm).wait_recv()
        remote(kv_at(frm), kv_at(frm), fs.at[frm], kr.at[frm], mate).start()
        return carry

    lax.fori_loop(1, 8, q_send, 0)
    lax.fori_loop(1, 8, kv_pass, 0)

    def cnt_get(i, carry):
        o = lax.rem(me + i, PEERS)
        cp = remote(cntbuf, cntall.at[o], cs.at[o], cr.at[o], o)
        cp.wait_send()
        cp.wait_recv()
        return carry

    lax.fori_loop(1, PEERS, cnt_get, 0)
    starts = cntall[0, 0]
    ends = cntall[0, 1]
    for i in range(1, PEERS):
        starts = starts + cntall[i, 0]
        ends = ends + cntall[i, 1]
    starts = starts.astype(jnp.int32)
    ends = ends.astype(jnp.int32)
    far = 2 * TOTAL
    q_starts = jnp.where((doc >= 1) & (doc < DOCS), starts, far)
    q_ends = jnp.where(doc < DOCS - 1, ends, far)

    ahead = lax.broadcasted_iota(jnp.int32, (pad, 128), 1) == 0
    docl[:pad] = jnp.where(ahead, 1.0, 0.0).astype(bf16)
    row_256 = lax.broadcasted_iota(jnp.int32, (256, 128), 0)

    def fill(j, carry):
        at = pl.ds(pl.multiple_of(j * 256 + pad, 256), 256)
        docl[at] = jnp.where(row_256 + j * 256 < starts, 1.0, 0.0).astype(bf16)
        return carry

    lax.fori_loop(0, TOTAL // 256, fill, 0)

    def kv_get(i, carry):
        frm = lax.rem(mate + 2 * i, PEERS)
        remote(kvbuf.at[0], kv_at(frm), ks.at[frm], kr.at[frm], frm).wait_recv()
        return carry

    lax.fori_loop(0, 8, kv_get, 0)
    own_kv.wait()

    lane = lax.broadcasted_iota(jnp.int32, (1, LANES), 1)
    sink = jnp.where(lane < TILE, sink_ref[head], sink_ref[head + 1])
    row = lax.broadcasted_iota(jnp.int32, (TILE, 128), 0)
    causal = lax.broadcasted_iota(jnp.int32, (UNIT, LANES), 0) <= (lane & (TILE - 1))
    nt = (((1,), (1,)), ((), ()))
    tn = (((0,), (0,)), ((), ()))

    def q_wait(frm):
        @pl.when(frm == me)
        def _():
            q_copies(me, frm, lambda *p: here(*p).wait())

        @pl.when(frm != me)
        def _():
            q_copies(me, frm, lambda *p: remote(*p, frm).wait_recv())

    def dq_copies(to, frm, go):
        fy, fz, fc = spot(frm)
        cols = pl.ds(pl.multiple_of(fz * 512 + fy * 128, 128), 128)

        def each(full, size):
            @pl.when(is_full(to, fc) == full)
            def _():
                dst, src = piece(to, full)
                take = pl.ds(pl.multiple_of(src, 64), size)
                rows = pl.ds(pl.multiple_of(dst, 64), size)
                go(dqb.at[take], dqo_ref.at[rows, cols], ds.at[to], dr.at[frm])

        each(1, TILE)
        each(0, TILE // 2)

    def dq_send(to):
        @pl.when(to == me)
        def _():
            dq_copies(to, me, lambda *p: here(*p).start())

        @pl.when(to != me)
        def _():
            dq_copies(to, me, lambda *p: remote(*p, to).start())

    first_tile = (3 * chip + 1 - c) // 2

    def tile(i, carry):
        t = lax.rem(first_tile + i, TILES)
        n0 = pl.multiple_of(t * TILE, TILE)
        place = 2 * t + c
        p0 = place * TILE
        third = lax.rem(place, 3)
        src = 2 * (place // 3)
        pl.when(third <= 1)(lambda: q_wait(src))
        pl.when(third >= 1)(lambda: q_wait(src + 1))

        qt = (ql[pl.ds(n0, TILE), :].astype(f32) * 0.125).astype(bf16)
        gt = gl[pl.ds(n0, TILE), :]
        none = jnp.zeros((TILE, D), bf16)
        w_ref[:TILE] = jnp.concatenate([qt[:, :D], none], axis=1)
        w_ref[TILE : 2 * TILE] = jnp.concatenate([qt[:, D:], none], axis=1)
        w_ref[2 * TILE : 3 * TILE] = jnp.concatenate([none, gt[:, :D]], axis=1)
        w_ref[3 * TILE :] = jnp.concatenate([none, gt[:, D:]], axis=1)
        inside = (row + p0 >= q_starts) & (row + p0 < q_ends)
        doc_ref[...] = jnp.where((doc == 0) | inside, FILL, 0.0).astype(bf16)

        def run(size):
            wg = w_ref[2 * TILE :]
            docs = jnp.concatenate([doc_ref[...]] * 2, axis=0)
            wq = jnp.concatenate([w_ref[: 2 * TILE], docs], axis=1)
            u0 = place + 1 - size + PAD

            def rows(i):
                return pl.ds(pl.multiple_of((u0 + i) * UNIT, UNIT), SUB * UNIT)

            subs = list(range(0, size, SUB))[::-1]
            top = sink
            mass = jnp.zeros((8, LANES), f32)
            tops = {}
            for i in subs:
                kv = kvl[rows(i), :]
                at = slice(i * UNIT, (i + SUB) * UNIT)
                kvd = jnp.concatenate([kv, docl[rows(i), :]], axis=1)
                s = lax.dot_general(kvd, wq, nt, preferred_element_type=f32)
                dp_ref[at, :] = lax.dot_general(kv, wg, nt, preferred_element_type=f32)
                if i + SUB == size:
                    s = jnp.concatenate(
                        [s[:-UNIT], jnp.where(causal, s[-UNIT:], FILL)], axis=0
                    )
                new = jnp.maximum(top, jnp.max(fold(s, jnp.max), axis=0, keepdims=True))
                e = jnp.exp2((s - new) * LOG2E)
                s_ref[at, :] = e
                mass = mass * jnp.exp2((top - new) * LOG2E) + fold(e, jnp.sum)
                top = tops[i] = new
            sink_e = jnp.exp2((sink - top) * LOG2E)
            inv = 1.0 / (jnp.sum(mass, axis=0, keepdims=True) + sink_e)

            delta = jnp.zeros((8, LANES), f32)
            scale = {}
            for i in subs:
                at = slice(i * UNIT, (i + SUB) * UNIT)
                scale[i] = jnp.exp2((tops[i] - top) * LOG2E) * inv
                prob_half = (s_ref[at, :] * scale[i]).astype(bf16).astype(f32)
                delta = delta + fold(prob_half * dp_ref[at, :], jnp.sum)
            delta = jnp.sum(delta, axis=0, keepdims=True)
            gacc_ref[...] += sink_e * inv * delta

            dq = jnp.zeros((LANES, 128), f32)
            w = w_ref[...]
            for i in subs:
                at = slice(i * UNIT, (i + SUB) * UNIT)
                prob = s_ref[at, :] * scale[i]
                dscore = (prob * (dp_ref[at, :] - delta)).astype(bf16)
                x = jnp.concatenate([dscore, prob.astype(bf16)], axis=1)
                acc_ref[rows(i), :] += jnp.dot(x, w, preferred_element_type=f32)
                dq = dq + lax.dot_general(dscore, kvl[rows(i), :], tn, preferred_element_type=f32)
            dq = dq[:, :D] * 0.125
            dq = jnp.concatenate([dq[:TILE], dq[TILE:]], axis=1)
            dqb[pl.ds(n0, TILE), :] = dq.astype(bf16)

        need = 2 * t + 2
        for over, size in zip((0,) + SIZES[:-1], SIZES):
            fits = (need > over) & (need <= size) if size < SIZES[-1] else need > over
            pl.when(fits)(functools.partial(run, size))
        pl.when(third <= 1)(lambda: dq_send(src))
        pl.when(third >= 1)(lambda: dq_send(src + 1))
        return carry

    lax.fori_loop(0, TILES, tile, 0)

    def block(b, core):
        return pl.ds(pl.multiple_of((2 * b + core) * ROWS + pad, 64), ROWS)

    def mate_send(i, carry):
        b = lax.rem(2 * y + z + 8 - i, 8)
        half[b] = acc_ref[block(b, 1 - c), :].astype(bf16)
        remote(half.at[b], mine.at[b], ms.at[b], mr.at[b], mate).start()
        return carry

    lax.fori_loop(1, 9, mate_send, 0)

    g = gacc_ref[...]
    ga = -jnp.sum(g[:, :TILE], axis=1, keepdims=True)
    gb = -jnp.sum(g[:, TILE:], axis=1, keepdims=True)
    g_row = jnp.where(doc == head, ga, jnp.where(doc == head + 1, gb, 0.0))
    gbuf[...] = g_row
    gall[me] = g_row

    def g_send(i, carry):
        to = lax.rem(me + i, PEERS)
        remote(gbuf, gall.at[me], es.at[to], er.at[me], to).start()
        return carry

    lax.fori_loop(1, PEERS, g_send, 0)

    def chip_sum(b):
        remote(half.at[b], mine.at[b], ms.at[b], mr.at[b], mate).wait_recv()
        return (acc_ref[block(b, c), :] + mine[b].astype(f32)).astype(bf16)

    def sum_send(i, carry):
        b = lax.rem(2 * y + z + 8 - i, 8)
        sums[b] = chip_sum(b)
        to = 2 * b + c
        remote(sums.at[b], land.at[2 * y + z], ss.at[b], sr.at[2 * y + z], to).start()
        return carry

    lax.fori_loop(1, 8, sum_send, 0)
    land[2 * y + z] = chip_sum(2 * y + z)

    def kv_sent(i, carry):
        to = lax.rem(me + 2 * i, PEERS)
        remote(kvbuf.at[0], kv_at(me), ks.at[to], kr.at[me], to).wait_send()
        remote(kv_at(to), kv_at(to), fs.at[to], kr.at[to], mate).wait_send()
        return carry

    lax.fori_loop(1, 8, kv_sent, 0)
    remote(kvbuf.at[0], kv_at(me), ks.at[mate], kr.at[me], mate).wait_send()

    def mate_sent(b, carry):
        remote(half.at[b], mine.at[b], ms.at[b], mr.at[b], mate).wait_send()
        return carry

    lax.fori_loop(0, 8, mate_sent, 0)

    def rest(i, carry):
        o = lax.rem(me + i, PEERS)
        q_copies(o, me, lambda *p: remote(*p, o).wait_send())
        dq_copies(o, me, lambda *p: remote(*p, o).wait_send())
        dq_copies(me, o, lambda *p: remote(*p, o).wait_recv())
        cp = remote(gbuf, gall.at[o], es.at[o], er.at[o], o)
        cp.wait_send()
        cp.wait_recv()
        return carry

    lax.fori_loop(1, PEERS, rest, 0)
    dq_copies(me, me, lambda *p: here(*p).wait())
    total = gall[0]
    for i in range(1, PEERS):
        total = total + gall[i]
    gso_ref[...] = total

    def sum_get(i, carry):
        b = lax.rem(2 * y + z + i, 8)
        cp = remote(sums.at[b], land.at[b], ss.at[b], sr.at[b], 2 * b + c)
        cp.wait_send()
        cp.wait_recv()
        return carry

    lax.fori_loop(1, 8, sum_get, 0)
    heads = []
    for h in range(2):
        heads.append(
            (land[h].astype(f32) + land[2 + h].astype(f32))
            + (land[4 + h].astype(f32) + land[6 + h].astype(f32))
        )
    dk_ref[...] = jnp.concatenate([heads[0][:, :D], heads[1][:, :D]], axis=1).astype(bf16)
    dv_ref[...] = jnp.concatenate([heads[0][:, D:], heads[1][:, D:]], axis=1).astype(bf16)


def whole(q, g, k, v, seg, sinks):
    any_ = pl.BlockSpec(memory_space=pl.ANY)
    vmem = pl.BlockSpec(memory_space=pltpu.VMEM)
    smem = pl.BlockSpec(memory_space=pltpu.SMEM)
    sem = pltpu.SemaphoreType.DMA
    blocks = pltpu.VMEM((8, ROWS, 128), bf16)
    longest = SIZES[-1] * UNIT
    return pl.pallas_call(
        whole_kernel,
        name="whole",
        out_shape=(
            jax.ShapeDtypeStruct((ROWS, 1024), bf16),
            jax.ShapeDtypeStruct((ROWS, 128), bf16),
            jax.ShapeDtypeStruct((ROWS, 128), bf16),
            jax.ShapeDtypeStruct((1, 128), f32),
        ),
        in_specs=[any_, any_, vmem, vmem, vmem, smem],
        out_specs=(any_, vmem, vmem, vmem),
        scratch_shapes=[
            pltpu.VMEM((2, ROWS, 128), bf16),
            pltpu.VMEM((2, 1, 128), f32),
            pltpu.VMEM((PEERS, 2, 1, 128), f32),
            pltpu.VMEM((TOTAL // 2, 128), bf16),
            pltpu.VMEM((TOTAL // 2, 128), bf16),
            pltpu.VMEM((PADDED, 128), bf16),
            pltpu.VMEM((PADDED, 128), bf16),
            pltpu.VMEM((PADDED, 128), f32),
            pltpu.VMEM((longest, LANES), f32),
            pltpu.VMEM((longest, LANES), f32),
            pltpu.VMEM((1, LANES), f32),
            pltpu.VMEM((4 * TILE, 128), bf16),
            pltpu.VMEM((TILE, 128), bf16),
            pltpu.VMEM((TOTAL // 2, 128), bf16),
            blocks,
            blocks,
            blocks,
            blocks,
            pltpu.VMEM((1, 128), f32),
            pltpu.VMEM((PEERS, 1, 128), f32),
        ]
        + [sem((PEERS,))] * 13
        + [sem((8,))] * 4
        + [sem((1,))],
        compiler_params=pltpu.CompilerParams(
            collective_id=0, has_side_effects=True, vmem_limit_bytes=32 * 1024 * 1024
        ),
    )(q, g, k, v, seg, sinks)


def on_device(queries, keys, values, grad_out, segments, sinks):
    grad_q, dk, dv, grad_sinks = whole(
        queries, grad_out, keys, values, segments.reshape(1, ROWS), sinks
    )
    return grad_q, dk, dv, grad_sinks.reshape(128)[: sinks.shape[0]]


def solution(mesh):
    rows = P(("dp", "ctx"), "tp")
    return jax.shard_map(
        on_device,
        mesh=mesh,
        in_specs=(rows, rows, rows, rows, P(("dp", "ctx")), P("tp")),
        out_specs=(rows, rows, rows, P(("dp", "tp"))),
        check_vma=False,
    )
```

time: 74.3 us -> 60.2 us (0.81)
  Pallas kernels: 66.2 us -> 52.5 us
    pallas_call x4 -> x1, Pallas kernels: 66.2 us -> 52.5 us  [whole(): pl.pallas_call(whole_kernel, name='whole', out_shape=(jax.ShapeDtypeStruc...]
    unnamed x18 -> x15, local copies, waits for them, and re-layouts: 6.55 us -> 6.25 us
where the time goes in v3:
time: 60.2 us; the launch traced here: 59.9 us
  Pallas kernels  52.5 us (87%)
  local copies, waits for them, and re-layouts  6.76 us (11%)
  between operations  0.66 us (1%)
    pallas_call x1, Pallas kernels, whole(): pl.pallas_call(whole_kernel, name='whole', out_shape=(jax.ShapeDtypeStruc...  52.5 us
    unnamed x15, local copies, waits for them, and re-layouts  6.25 us

profile of v3, /device:TPU:1, one launch (start us, length us, event | category | flops | bytes accessed | tf_op | source)
XLA Modules:
  0.0 59.9 jit_solution(8097779035070087566)
XLA Ops:
  0.6 0.0 copy-start.5
  0.6 0.0 copy-start.4
  0.7 0.6 %copy-done.5 = f32[16]{0:T(128)S(1)} copy-done((f32[16]{0:T(128)S(1)}, f32[16]{0:T(128)}, u32[]{:S(2)}) %copy-start.5) | copy-done | bytes 88
  1.3 0.0 copy-done.4
  1.3 0.0 copy-start
  1.3 1.0 %copy-done = bf16[192,1024]{1,0:T(8,128)(2,1)S(1)} copy-done((bf16[192,1024]{1,0:T(8,128)(2,1)S(1)}, bf16[192,1024]{1,0:T(8,128)(2,1)}, u32[]{:S(2)}) %copy-start) | copy-done | bytes 393240
  2.3 0.0 copy-start.1
  2.3 1.0 %copy-done.1 = bf16[192,1024]{1,0:T(8,128)(2,1)S(1)} copy-done((bf16[192,1024]{1,0:T(8,128)(2,1)S(1)}, bf16[192,1024]{1,0:T(8,128)(2,1)}, u32[]{:S(2)}) %copy-start.1) | copy-done | bytes 393240
  3.3 0.0 copy-start.2
  3.3 0.8 %copy-done.2 = bf16[192,128]{1,0:T(8,128)(2,1)S(1)} copy-done((bf16[192,128]{1,0:T(8,128)(2,1)S(1)}, bf16[192,128]{1,0:T(8,128)(2,1)}, u32[]{:S(2)}) %copy-start.2) | copy-done | bytes 49176
  4.1 0.0 copy-start.3
  4.1 0.8 %copy-done.3 = bf16[192,128]{1,0:T(8,128)(2,1)S(1)} copy-done((bf16[192,128]{1,0:T(8,128)(2,1)S(1)}, bf16[192,128]{1,0:T(8,128)(2,1)}, u32[]{:S(2)}) %copy-start.3) | copy-done | bytes 49176
  4.9 52.5 %whole.1 = (bf16[192,1024]{1,0:T(8,128)(2,1)S(1)}, bf16[192,128]{1,0:T(8,128)(2,1)S(1)}, bf16[192,128]{1,0:T(8,128)(2,1)S(1)}, f32[1,128]{1,0:T(1,128)S(1)}) custom-call(bf16[192,1024]{1,0:T(8,128)(2,1)S(1)} %copy-done, bf16[192,1024]{1,0:T(8,128)(2,1)S(1)} %copy-done.1, bf16[192,128]{1,0:T(8,128)(2,1)S(1)} %copy-done.2, bf16[192,128]{1,0:T(8,128)(2,1)S(1)} %copy-done.3, ...), custom_call_target="tpu_custom_call" | custom-call | tf_op jit(solution)/shard_map/whole/pallas_call | solution.py:426
  57.4 0.5 slice_bitcast_fusion
  57.9 0.7 %copy.13 = bf16[192,1024]{1,0:T(8,128)(2,1)} copy(bf16[192,1024]{1,0:T(8,128)(2,1)S(1)} %get-tuple-element.16) | data formatting | bytes 786432
  58.7 0.6 %copy.14 = bf16[192,128]{1,0:T(8,128)(2,1)} copy(bf16[192,128]{1,0:T(8,128)(2,1)S(1)} %get-tuple-element.17) | data formatting | bytes 98304
  59.3 0.6 %copy.15 = bf16[192,128]{1,0:T(8,128)(2,1)} copy(bf16[192,128]{1,0:T(8,128)(2,1)S(1)} %get-tuple-element.18) | data formatting | bytes 98304
Async XLA Ops:
  0.6 0.7 %copy-start.5 = (f32[16]{0:T(128)S(1)}, f32[16]{0:T(128)}, u32[]{:S(2)}) copy-start(f32[16]{0:T(128)} %sink_ref.1) | copy-start | bytes 196
  0.6 0.7 %copy-start.4 = (s32[192]{0:T(256)S(1)}, s32[192]{0:T(256)}, u32[]{:S(2)}) copy-start(s32[192]{0:T(256)} %param.10) | copy-start | bytes 2308
  1.3 1.0 %copy-start = (bf16[192,1024]{1,0:T(8,128)(2,1)S(1)}, bf16[192,1024]{1,0:T(8,128)(2,1)}, u32[]{:S(2)}) copy-start(bf16[192,1024]{1,0:T(8,128)(2,1)} %q_ref.1) | copy-start | bytes 1179652
  2.3 1.0 %copy-start.1 = (bf16[192,1024]{1,0:T(8,128)(2,1)S(1)}, bf16[192,1024]{1,0:T(8,128)(2,1)}, u32[]{:S(2)}) copy-start(bf16[192,1024]{1,0:T(8,128)(2,1)} %g_ref.1) | copy-start | bytes 1179652
  3.3 0.8 %copy-start.2 = (bf16[192,128]{1,0:T(8,128)(2,1)S(1)}, bf16[192,128]{1,0:T(8,128)(2,1)}, u32[]{:S(2)}) copy-start(bf16[192,128]{1,0:T(8,128)(2,1)} %k_ref.1) | copy-start | bytes 147460
  4.1 0.8 %copy-start.3 = (bf16[192,128]{1,0:T(8,128)(2,1)S(1)}, bf16[192,128]{1,0:T(8,128)(2,1)}, u32[]{:S(2)}) copy-start(bf16[192,128]{1,0:T(8,128)(2,1)} %v_ref.1) | copy-start | bytes 147460

commit v4 on v3

--- a/solution.py
+++ b/solution.py
@@ -20,6 +20,7 @@
 PAD = 4
 PADDED = TOTAL + PAD * UNIT
 SIZES = (2, 4, 8, 12, 16, 20)
+GRANT = 63 * 1024 * 1024
 LOG2E = 1.4426950408889634
 FILL = -1e30
 f32 = jnp.float32
@@ -58,17 +59,17 @@
 
 
 def greet(me):
-    barrier = pltpu.get_barrier_semaphore()
-
     def hello(i, carry):
         to = lax.rem(me + i, PEERS)
         pl.semaphore_signal(
-            barrier, inc=1, device_id={"ctx": to}, device_id_type=pl.DeviceIdType.MESH
+            pltpu.get_barrier_semaphore(),
+            inc=1,
+            device_id={"ctx": to},
+            device_id_type=pl.DeviceIdType.MESH,
         )
         return carry
 
     lax.fori_loop(1, PEERS, hello, 0)
-    pl.semaphore_wait(barrier, PEERS - 1)
 
 
 def fold(x, op):
@@ -76,9 +77,9 @@
 
 
 def whole_kernel(
-    q_ref, g_ref, k_ref, v_ref, seg_ref, sink_ref,
+    q_ref, g_ref, k_hbm, v_hbm, seg_hbm, sink_hbm,
     dqo_ref, dk_ref, dv_ref, gso_ref,
-    kvbuf, cntbuf, cntall, ql, gl, kvl, docl, acc_ref, s_ref, dp_ref, gacc_ref, w_ref, doc_ref,
+    k_ref, v_ref, seg_ref, sink_ref, kvbuf, cntbuf, cntall, ql, gl, kvl, docl, acc_ref, s_ref, dp_ref, gacc_ref, w_ref, doc_ref,
     dqb, half, mine, sums, land, gbuf, gall,
     ks, kr, fs, cs, cr, qs, qr, gs, gr, ds, dr, es, er, ms, mr, ss, sr, ls,
 ):
@@ -88,6 +89,21 @@
     mate = me + 1 - 2 * c
     head = 8 * z + 2 * y
     pad = PAD * UNIT
+
+    greet(me)
+    fetch = [
+        pltpu.make_async_copy(src, dst, ls.at[1 + i])
+        for i, (src, dst) in enumerate(
+            [(k_hbm, k_ref), (v_hbm, v_ref), (seg_hbm, seg_ref), (sink_hbm, sink_ref)]
+        )
+    ]
+    for f in fetch:
+        f.start()
+    acc_ref[...] = jnp.zeros_like(acc_ref)
+    gacc_ref[...] = jnp.zeros_like(gacc_ref)
+    kvl[:pad] = jnp.zeros((pad, 128), bf16)
+    for f in fetch:
+        f.wait()
 
     for h in range(2):
         kvbuf[h] = jnp.concatenate(
@@ -103,7 +119,7 @@
         cntbuf[i] = counts[i]
         cntall[me, i] = counts[i]
 
-    greet(me)
+    pl.semaphore_wait(pltpu.get_barrier_semaphore(), PEERS - 1)
 
     def kv_at(i):
         return kvl.at[pl.ds(pl.multiple_of(i * ROWS + pad, 64), ROWS)]
@@ -142,11 +158,6 @@
     lax.fori_loop(1, PEERS, cnt_send, 0)
     q_copies(me, me, lambda *p: here(*p).start())
     q_copies(mate, me, lambda *p: remote(*p, mate).start())
-
-    acc_ref[...] = jnp.zeros_like(acc_ref)
-    gacc_ref[...] = jnp.zeros_like(gacc_ref)
-    kvl[:pad] = jnp.zeros((pad, 128), bf16)
-    w_ref[...] = jnp.zeros_like(w_ref)
 
     def q_send(i, carry):
         for core in range(2):
@@ -396,7 +407,7 @@
     total = gall[0]
     for i in range(1, PEERS):
         total = total + gall[i]
-    gso_ref[...] = total
+    gso_ref[...] = total[0, :16]
 
     def sum_get(i, carry):
         b = lax.rem(2 * y + z + i, 8)
@@ -417,9 +428,8 @@
 
 
 def whole(q, g, k, v, seg, sinks):
-    any_ = pl.BlockSpec(memory_space=pl.ANY)
+    hbm = pl.BlockSpec(memory_space=pltpu.HBM)
     vmem = pl.BlockSpec(memory_space=pltpu.VMEM)
-    smem = pl.BlockSpec(memory_space=pltpu.SMEM)
     sem = pltpu.SemaphoreType.DMA
     blocks = pltpu.VMEM((8, ROWS, 128), bf16)
     longest = SIZES[-1] * UNIT
@@ -430,11 +440,15 @@
             jax.ShapeDtypeStruct((ROWS, 1024), bf16),
             jax.ShapeDtypeStruct((ROWS, 128), bf16),
             jax.ShapeDtypeStruct((ROWS, 128), bf16),
-            jax.ShapeDtypeStruct((1, 128), f32),
+            jax.ShapeDtypeStruct((16,), f32),
         ),
-        in_specs=[any_, any_, vmem, vmem, vmem, smem],
-        out_specs=(any_, vmem, vmem, vmem),
+        in_specs=[hbm] * 6,
+        out_specs=(hbm, vmem, vmem, vmem),
         scratch_shapes=[
+            pltpu.VMEM((ROWS, 128), bf16),
+            pltpu.VMEM((ROWS, 128), bf16),
+            pltpu.VMEM((1, ROWS), jnp.int32),
+            pltpu.SMEM((16,), f32),
             pltpu.VMEM((2, ROWS, 128), bf16),
             pltpu.VMEM((2, 1, 128), f32),
             pltpu.VMEM((PEERS, 2, 1, 128), f32),
@@ -458,18 +472,58 @@
         ]
         + [sem((PEERS,))] * 13
         + [sem((8,))] * 4
-        + [sem((1,))],
+        + [sem((5,))],
         compiler_params=pltpu.CompilerParams(
-            collective_id=0, has_side_effects=True, vmem_limit_bytes=32 * 1024 * 1024
+            collective_id=0, has_side_effects=True, vmem_limit_bytes=GRANT
         ),
     )(q, g, k, v, seg, sinks)
+
+
+def hand_over_kernel(*refs):
+    sems = refs[-2:]
+    n = (len(refs) - 2) // 3
+    moves = []
+    for i in range(n):
+        src, dst, via = refs[i], refs[n + i], refs[2 * n + i]
+        parts = [pl.ds(r, 48) for r in range(0, ROWS, 48)] if src.shape[1:] == (1024,) else [None]
+        for part in parts:
+            ref = [r if part is None else r.at[part] for r in (src, via, dst)]
+            k = len(moves)
+            moves.append(
+                (
+                    pltpu.make_async_copy(ref[0], ref[1], sems[0].at[k]),
+                    pltpu.make_async_copy(ref[1], ref[2], sems[1].at[k]),
+                )
+            )
+    for come, _ in moves:
+        come.start()
+    for come, go in moves:
+        come.wait()
+        go.start()
+    for _, go in moves:
+        go.wait()
+
+
+def hand_over(*arrays):
+    hbm = pl.BlockSpec(memory_space=pltpu.HBM)
+    shapes = [(a.shape, a.dtype) for a in arrays]
+    return pl.pallas_call(
+        hand_over_kernel,
+        name="hand_over",
+        out_shape=tuple(jax.ShapeDtypeStruct(*a) for a in shapes),
+        in_specs=[hbm] * len(arrays),
+        out_specs=(hbm,) * len(arrays),
+        scratch_shapes=[pltpu.VMEM(*a) for a in shapes]
+        + [pltpu.SemaphoreType.DMA((16,))] * 2,
+        compiler_params=pltpu.CompilerParams(vmem_limit_bytes=GRANT),
+    )(*arrays)
 
 
 def on_device(queries, keys, values, grad_out, segments, sinks):
     grad_q, dk, dv, grad_sinks = whole(
         queries, grad_out, keys, values, segments.reshape(1, ROWS), sinks
     )
-    return grad_q, dk, dv, grad_sinks.reshape(128)[: sinks.shape[0]]
+    return hand_over(grad_q, dk, dv, grad_sinks)
 
 
 def solution(mesh):

time: 60.2 us -> 55.8 us (0.927)
  local copies, waits for them, and re-layouts: 6.76 us -> 0 us
  Pallas kernels: 52.5 us -> 55 us
    unnamed x15 -> x0, local copies, waits for them, and re-layouts: 6.25 us -> none
    pallas_call x0 -> x1, Pallas kernels: none -> 1.99 us  [hand_over(): pl.pallas_call(hand_over_kernel, name='hand_over', out_shape=tuple((jax.S...]
where the time goes in v4:
time: 55.8 us; the launch traced here: 55.6 us
  Pallas kernels  55 us (99%)
  between operations  0.64 us (1%)
    pallas_call x1, Pallas kernels, whole(): pl.pallas_call(whole_kernel, name='whole', out_shape=(jax.ShapeDtypeStruc...  53 us
    pallas_call x1, Pallas kernels, hand_over(): pl.pallas_call(hand_over_kernel, name='hand_over', out_shape=tuple((jax.S...  1.99 us

profile of v4, /device:TPU:1, one launch (start us, length us, event | category | flops | bytes accessed | tf_op | source)
XLA Modules:
  0.0 55.6 jit_solution(4448694366983226162)
XLA Ops:
  0.6 53.0 %whole.1 = (bf16[192,1024]{1,0:T(8,128)(2,1)}, bf16[192,128]{1,0:T(8,128)(2,1)}, bf16[192,128]{1,0:T(8,128)(2,1)}, f32[16]{0:T(128)}) custom-call(bf16[192,1024]{1,0:T(8,128)(2,1)} %q_ref.1, bf16[192,1024]{1,0:T(8,128)(2,1)} %g_ref.1, bf16[192,128]{1,0:T(8,128)(2,1)} %k_hbm.1, bf16[192,128]{1,0:T(8,128)(2,1)} %v_hbm.1, s32[1,192]{1,0:T(1,128)} %bitcast.1, ...), custom_call_target="tpu_custom_call" | custom-call | tf_op jit(solution)/shard_map/whole/pallas_call | solution.py:436
  53.6 2.0 %hand_over.1 = (bf16[192,1024]{1,0:T(8,128)(2,1)}, bf16[192,128]{1,0:T(8,128)(2,1)}, bf16[192,128]{1,0:T(8,128)(2,1)}, f32[16]{0:T(128)}) custom-call(bf16[192,1024]{1,0:T(8,128)(2,1)} %get-tuple-element.8.refs_0_, bf16[192,128]{1,0:T(8,128)(2,1)} %get-tuple-element.9.refs_1_, bf16[192,128]{1,0:T(8,128)(2,1)} %get-tuple-element.10.refs_2_, ...), custom_call_target="tpu_custom_call" | custom-call | tf_op jit(solution)/shard_map/hand_over/pallas_call | solution.py:510

commit v5 on v4

--- a/solution.py
+++ b/solution.py
@@ -19,7 +19,7 @@
 SUB = 2
 PAD = 4
 PADDED = TOTAL + PAD * UNIT
-SIZES = (2, 4, 8, 12, 16, 20)
+LONGEST = 20
 GRANT = 63 * 1024 * 1024
 LOG2E = 1.4426950408889634
 FILL = -1e30
@@ -159,10 +159,18 @@
     q_copies(me, me, lambda *p: here(*p).start())
     q_copies(mate, me, lambda *p: remote(*p, mate).start())
 
+    whole_core = lax.rem((3 * me + c) // 2, 2)
+    shares = ((TILE, whole_core, *piece(me, 1)), (TILE // 2, 1 - whole_core, *piece(me, 0)))
+
     def q_send(i, carry):
-        for core in range(2):
-            to = lax.rem(2 * chip + PEERS - 2 * i, PEERS) + core
-            q_copies(to, me, lambda *p: remote(*p, to).start())
+        ch = lax.rem(chip + 8 - i, 8)
+        cols = pl.ds(pl.multiple_of(lax.rem(ch, 2) * 512 + (ch // 2) * 128, 128), 128)
+        for size, core, src, dst in shares:
+            to = 2 * ch + core
+            rows = pl.ds(pl.multiple_of(src, 64), size)
+            at = pl.ds(pl.multiple_of(dst, 64), size)
+            remote(q_ref.at[rows, cols], ql.at[at], qs.at[to], qr.at[me], to).start()
+            remote(g_ref.at[rows, cols], gl.at[at], gs.at[to], gr.at[me], to).start()
         return carry
 
     def kv_pass(i, carry):
@@ -219,14 +227,15 @@
     nt = (((1,), (1,)), ((), ()))
     tn = (((0,), (0,)), ((), ()))
 
-    def q_wait(frm):
-        @pl.when(frm == me)
-        def _():
-            q_copies(me, frm, lambda *p: here(*p).wait())
+    q_copies(me, me, lambda *p: here(*p).wait())
+
+    def q_wait(frm, size, *_):
+        some = pl.ds(0, size)
 
         @pl.when(frm != me)
         def _():
-            q_copies(me, frm, lambda *p: remote(*p, frm).wait_recv())
+            remote(q_ref.at[some, :128], ql.at[some], qs.at[frm], qr.at[frm], frm).wait_recv()
+            remote(g_ref.at[some, :128], gl.at[some], gs.at[frm], gr.at[frm], frm).wait_recv()
 
     def dq_copies(to, frm, go):
         fy, fz, fc = spot(frm)
@@ -243,100 +252,138 @@
         each(1, TILE)
         each(0, TILE // 2)
 
-    def dq_send(to):
+    my_cols = pl.ds(pl.multiple_of(z * 512 + y * 128, 128), 128)
+
+    def dq_send(to, size, row, src):
+        p = (
+            dqb.at[pl.ds(pl.multiple_of(src, 64), size)],
+            dqo_ref.at[pl.ds(row, size), my_cols],
+            ds.at[to],
+            dr.at[me],
+        )
+
         @pl.when(to == me)
         def _():
-            dq_copies(to, me, lambda *p: here(*p).start())
+            here(*p).start()
 
         @pl.when(to != me)
         def _():
-            dq_copies(to, me, lambda *p: remote(*p, to).start())
-
-    first_tile = (3 * chip + 1 - c) // 2
-
-    def tile(i, carry):
-        t = lax.rem(first_tile + i, TILES)
-        n0 = pl.multiple_of(t * TILE, TILE)
+            remote(*p, to).start()
+
+    first_pair = (3 * chip + 3) // 4
+
+    def sources(t, act):
         place = 2 * t + c
-        p0 = place * TILE
         third = lax.rem(place, 3)
         src = 2 * (place // 3)
-        pl.when(third <= 1)(lambda: q_wait(src))
-        pl.when(third >= 1)(lambda: q_wait(src + 1))
-
+        n0 = t * TILE
+
+        @pl.when(third == 0)
+        def _():
+            act(src, TILE, 0, n0)
+
+        @pl.when(third == 1)
+        def _():
+            act(src, TILE // 2, TILE, n0)
+            act(src + 1, TILE // 2, 0, n0 + TILE // 2)
+
+        @pl.when(third == 2)
+        def _():
+            act(src + 1, TILE, TILE // 2, n0)
+
+    def ready(k, t):
+        n0 = pl.multiple_of(t * TILE, TILE)
+        p0 = (2 * t + c) * TILE
         qt = (ql[pl.ds(n0, TILE), :].astype(f32) * 0.125).astype(bf16)
         gt = gl[pl.ds(n0, TILE), :]
         none = jnp.zeros((TILE, D), bf16)
-        w_ref[:TILE] = jnp.concatenate([qt[:, :D], none], axis=1)
-        w_ref[TILE : 2 * TILE] = jnp.concatenate([qt[:, D:], none], axis=1)
-        w_ref[2 * TILE : 3 * TILE] = jnp.concatenate([none, gt[:, :D]], axis=1)
-        w_ref[3 * TILE :] = jnp.concatenate([none, gt[:, D:]], axis=1)
+        w_ref[k, :TILE] = jnp.concatenate([qt[:, :D], none], axis=1)
+        w_ref[k, TILE : 2 * TILE] = jnp.concatenate([qt[:, D:], none], axis=1)
+        w_ref[k, 2 * TILE : 3 * TILE] = jnp.concatenate([none, gt[:, :D]], axis=1)
+        w_ref[k, 3 * TILE :] = jnp.concatenate([none, gt[:, D:]], axis=1)
         inside = (row + p0 >= q_starts) & (row + p0 < q_ends)
-        doc_ref[...] = jnp.where((doc == 0) | inside, FILL, 0.0).astype(bf16)
-
-        def run(size):
-            wg = w_ref[2 * TILE :]
-            docs = jnp.concatenate([doc_ref[...]] * 2, axis=0)
-            wq = jnp.concatenate([w_ref[: 2 * TILE], docs], axis=1)
-            u0 = place + 1 - size + PAD
-
-            def rows(i):
-                return pl.ds(pl.multiple_of((u0 + i) * UNIT, UNIT), SUB * UNIT)
-
-            subs = list(range(0, size, SUB))[::-1]
-            top = sink
-            mass = jnp.zeros((8, LANES), f32)
-            tops = {}
-            for i in subs:
-                kv = kvl[rows(i), :]
-                at = slice(i * UNIT, (i + SUB) * UNIT)
-                kvd = jnp.concatenate([kv, docl[rows(i), :]], axis=1)
-                s = lax.dot_general(kvd, wq, nt, preferred_element_type=f32)
-                dp_ref[at, :] = lax.dot_general(kv, wg, nt, preferred_element_type=f32)
-                if i + SUB == size:
-                    s = jnp.concatenate(
-                        [s[:-UNIT], jnp.where(causal, s[-UNIT:], FILL)], axis=0
-                    )
-                new = jnp.maximum(top, jnp.max(fold(s, jnp.max), axis=0, keepdims=True))
-                e = jnp.exp2((s - new) * LOG2E)
-                s_ref[at, :] = e
-                mass = mass * jnp.exp2((top - new) * LOG2E) + fold(e, jnp.sum)
-                top = tops[i] = new
-            sink_e = jnp.exp2((sink - top) * LOG2E)
-            inv = 1.0 / (jnp.sum(mass, axis=0, keepdims=True) + sink_e)
-
-            delta = jnp.zeros((8, LANES), f32)
-            scale = {}
-            for i in subs:
-                at = slice(i * UNIT, (i + SUB) * UNIT)
-                scale[i] = jnp.exp2((tops[i] - top) * LOG2E) * inv
-                prob_half = (s_ref[at, :] * scale[i]).astype(bf16).astype(f32)
-                delta = delta + fold(prob_half * dp_ref[at, :], jnp.sum)
-            delta = jnp.sum(delta, axis=0, keepdims=True)
-            gacc_ref[...] += sink_e * inv * delta
-
-            dq = jnp.zeros((LANES, 128), f32)
-            w = w_ref[...]
-            for i in subs:
-                at = slice(i * UNIT, (i + SUB) * UNIT)
-                prob = s_ref[at, :] * scale[i]
-                dscore = (prob * (dp_ref[at, :] - delta)).astype(bf16)
-                x = jnp.concatenate([dscore, prob.astype(bf16)], axis=1)
-                acc_ref[rows(i), :] += jnp.dot(x, w, preferred_element_type=f32)
-                dq = dq + lax.dot_general(dscore, kvl[rows(i), :], tn, preferred_element_type=f32)
-            dq = dq[:, :D] * 0.125
-            dq = jnp.concatenate([dq[:TILE], dq[TILE:]], axis=1)
-            dqb[pl.ds(n0, TILE), :] = dq.astype(bf16)
-
-        need = 2 * t + 2
-        for over, size in zip((0,) + SIZES[:-1], SIZES):
-            fits = (need > over) & (need <= size) if size < SIZES[-1] else need > over
-            pl.when(fits)(functools.partial(run, size))
-        pl.when(third <= 1)(lambda: dq_send(src))
-        pl.when(third >= 1)(lambda: dq_send(src + 1))
-        return carry
-
-    lax.fori_loop(0, TILES, tile, 0)
+        doc_ref[k] = jnp.where((doc == 0) | inside, FILL, 0.0).astype(bf16)
+
+    def chain(k, t, size):
+        wg = w_ref[k, 2 * TILE :]
+        docs = jnp.concatenate([doc_ref[k]] * 2, axis=0)
+        wq = jnp.concatenate([w_ref[k, : 2 * TILE], docs], axis=1)
+        u0 = 2 * t + c + 1 - size + PAD
+
+        def rows(i):
+            return pl.ds(pl.multiple_of((u0 + i) * UNIT, UNIT), SUB * UNIT)
+
+        subs = list(range(0, size, SUB))[::-1]
+        top = sink
+        mass = jnp.zeros((8, LANES), f32)
+        tops = {}
+        for i in subs:
+            kv = kvl[rows(i), :]
+            at = slice(i * UNIT, (i + SUB) * UNIT)
+            kvd = jnp.concatenate([kv, docl[rows(i), :]], axis=1)
+            s = lax.dot_general(kvd, wq, nt, preferred_element_type=f32)
+            dp_ref[k, at, :] = lax.dot_general(kv, wg, nt, preferred_element_type=f32)
+            if i + SUB == size:
+                s = jnp.concatenate([s[:-UNIT], jnp.where(causal, s[-UNIT:], FILL)], axis=0)
+            new = jnp.maximum(top, jnp.max(fold(s, jnp.max), axis=0, keepdims=True))
+            e = jnp.exp2((s - new) * LOG2E)
+            s_ref[k, at, :] = e
+            mass = mass * jnp.exp2((top - new) * LOG2E) + fold(e, jnp.sum)
+            top = tops[i] = new
+            yield
+        sink_e = jnp.exp2((sink - top) * LOG2E)
+        inv = 1.0 / (jnp.sum(mass, axis=0, keepdims=True) + sink_e)
+
+        delta = jnp.zeros((8, LANES), f32)
+        scale = {}
+        for i in subs:
+            at = slice(i * UNIT, (i + SUB) * UNIT)
+            scale[i] = jnp.exp2((tops[i] - top) * LOG2E) * inv
+            prob_half = (s_ref[k, at, :] * scale[i]).astype(bf16).astype(f32)
+            delta = delta + fold(prob_half * dp_ref[k, at, :], jnp.sum)
+            yield
+        delta = jnp.sum(delta, axis=0, keepdims=True)
+        gacc_ref[...] += sink_e * inv * delta
+
+        dq = jnp.zeros((LANES, 128), f32)
+        w = w_ref[k]
+        for i in subs:
+            at = slice(i * UNIT, (i + SUB) * UNIT)
+            prob = s_ref[k, at, :] * scale[i]
+            dscore = (prob * (dp_ref[k, at, :] - delta)).astype(bf16)
+            x = jnp.concatenate([dscore, prob.astype(bf16)], axis=1)
+            acc_ref[rows(i), :] += jnp.dot(x, w, preferred_element_type=f32)
+            dq = dq + lax.dot_general(dscore, kvl[rows(i), :], tn, preferred_element_type=f32)
+            yield
+        dq = dq[:, :D] * 0.125
+        dq = jnp.concatenate([dq[:TILE], dq[TILE:]], axis=1)
+        dqb[pl.ds(pl.multiple_of(t * TILE, TILE), TILE), :] = dq.astype(bf16)
+
+    def pair(i, carry):
+        p = lax.rem(first_pair + i, TILES // 2)
+        for k in range(2):
+            sources(2 * p + k, q_wait)
+            ready(k, 2 * p + k)
+
+        def run(n):
+            left = [chain(k, 2 * p + k, min(4 * n + 2 * k + 2, LONGEST)) for k in range(2)]
+            while left:
+                left = [steps for steps in left if next(steps, 0) is None]
+
+        for n in range(TILES // 2):
+            pl.when(p == n)(functools.partial(run, n))
+        for k in range(2):
+            sources(2 * p + k, dq_send)
+        return carry
+
+    lax.fori_loop(0, TILES // 2, pair, 0)
+
+    g = gacc_ref[...]
+    ga = -jnp.sum(g[:, :TILE], axis=1, keepdims=True)
+    gb = -jnp.sum(g[:, TILE:], axis=1, keepdims=True)
+    gbuf[0] = jnp.where(doc == head, ga, jnp.where(doc == head + 1, gb, 0.0))
+    g_mate = remote(gbuf.at[0], gbuf.at[1], es.at[8], er.at[8], mate)
+    g_mate.start()
 
     def block(b, core):
         return pl.ds(pl.multiple_of((2 * b + core) * ROWS + pad, 64), ROWS)
@@ -348,20 +395,6 @@
         return carry
 
     lax.fori_loop(1, 9, mate_send, 0)
-
-    g = gacc_ref[...]
-    ga = -jnp.sum(g[:, :TILE], axis=1, keepdims=True)
-    gb = -jnp.sum(g[:, TILE:], axis=1, keepdims=True)
-    g_row = jnp.where(doc == head, ga, jnp.where(doc == head + 1, gb, 0.0))
-    gbuf[...] = g_row
-    gall[me] = g_row
-
-    def g_send(i, carry):
-        to = lax.rem(me + i, PEERS)
-        remote(gbuf, gall.at[me], es.at[to], er.at[me], to).start()
-        return carry
-
-    lax.fori_loop(1, PEERS, g_send, 0)
 
     def chip_sum(b):
         remote(half.at[b], mine.at[b], ms.at[b], mr.at[b], mate).wait_recv()
@@ -377,6 +410,17 @@
     lax.fori_loop(1, 8, sum_send, 0)
     land[2 * y + z] = chip_sum(2 * y + z)
 
+    g_mate.wait()
+    gbuf[2] = gbuf[0] + gbuf[1]
+    gall[chip] = gbuf[2]
+
+    def g_send(i, carry):
+        ch = lax.rem(chip + i, 8)
+        remote(gbuf.at[2], gall.at[chip], es.at[ch], er.at[chip], 2 * ch + c).start()
+        return carry
+
+    lax.fori_loop(1, 8, g_send, 0)
+
     def kv_sent(i, carry):
         to = lax.rem(me + 2 * i, PEERS)
         remote(kvbuf.at[0], kv_at(me), ks.at[to], kr.at[me], to).wait_send()
@@ -392,20 +436,34 @@
 
     lax.fori_loop(0, 8, mate_sent, 0)
 
+    def dq_sent(ch, size):
+        some = pl.ds(0, size)
+        for core in range(2):
+            to = 2 * ch + core
+            remote(dqb.at[some], dqo_ref.at[some, my_cols], ds.at[to], dr.at[to], to).wait_send()
+
     def rest(i, carry):
-        o = lax.rem(me + i, PEERS)
-        q_copies(o, me, lambda *p: remote(*p, o).wait_send())
-        dq_copies(o, me, lambda *p: remote(*p, o).wait_send())
-        dq_copies(me, o, lambda *p: remote(*p, o).wait_recv())
-        cp = remote(gbuf, gall.at[o], es.at[o], er.at[o], o)
+        ch = lax.rem(chip + i, 8)
+        for size, core, _, _ in shares:
+            o = 2 * ch + core
+            some = pl.ds(0, size)
+            remote(q_ref.at[some, :128], ql.at[some], qs.at[o], qr.at[o], o).wait_send()
+            remote(g_ref.at[some, :128], gl.at[some], gs.at[o], gr.at[o], o).wait_send()
+            remote(dqb.at[some], dqo_ref.at[some, my_cols], ds.at[o], dr.at[o], o).wait_recv()
+        pl.when(lax.rem(ch + c, 2) == 0)(lambda: dq_sent(ch, TILE))
+        pl.when(lax.rem(ch + c, 2) == 1)(lambda: dq_sent(ch, TILE // 2))
+        cp = remote(gbuf.at[2], gall.at[ch], es.at[ch], er.at[ch], 2 * ch + c)
         cp.wait_send()
         cp.wait_recv()
         return carry
 
-    lax.fori_loop(1, PEERS, rest, 0)
+    lax.fori_loop(1, 8, rest, 0)
+    q_copies(mate, me, lambda *p: remote(*p, mate).wait_send())
+    dq_copies(mate, me, lambda *p: remote(*p, mate).wait_send())
+    dq_copies(me, mate, lambda *p: remote(*p, mate).wait_recv())
     dq_copies(me, me, lambda *p: here(*p).wait())
     total = gall[0]
-    for i in range(1, PEERS):
+    for i in range(1, 8):
         total = total + gall[i]
     gso_ref[...] = total[0, :16]
 
@@ -432,7 +490,7 @@
     vmem = pl.BlockSpec(memory_space=pltpu.VMEM)
     sem = pltpu.SemaphoreType.DMA
     blocks = pltpu.VMEM((8, ROWS, 128), bf16)
-    longest = SIZES[-1] * UNIT
+    longest = LONGEST * UNIT
     return pl.pallas_call(
         whole_kernel,
         name="whole",
@@ -457,18 +515,18 @@
             pltpu.VMEM((PADDED, 128), bf16),
             pltpu.VMEM((PADDED, 128), bf16),
             pltpu.VMEM((PADDED, 128), f32),
-            pltpu.VMEM((longest, LANES), f32),
-            pltpu.VMEM((longest, LANES), f32),
+            pltpu.VMEM((2, longest, LANES), f32),
+            pltpu.VMEM((2, longest, LANES), f32),
             pltpu.VMEM((1, LANES), f32),
-            pltpu.VMEM((4 * TILE, 128), bf16),
-            pltpu.VMEM((TILE, 128), bf16),
+            pltpu.VMEM((2, 4 * TILE, 128), bf16),
+            pltpu.VMEM((2, TILE, 128), bf16),
             pltpu.VMEM((TOTAL // 2, 128), bf16),
             blocks,
             blocks,
             blocks,
             blocks,
-            pltpu.VMEM((1, 128), f32),
-            pltpu.VMEM((PEERS, 1, 128), f32),
+            pltpu.VMEM((3, 1, 128), f32),
+            pltpu.VMEM((8, 1, 128), f32),
         ]
         + [sem((PEERS,))] * 13
         + [sem((8,))] * 4

time: 55.8 us -> 54.8 us (0.982)
  Pallas kernels: 55 us -> 53.9 us
    pallas_call x1, Pallas kernels: 53 us -> 51.9 us  [whole(): pl.pallas_call(whole_kernel, name='whole', out_shape=(jax.ShapeDtypeStruc...]
where the time goes in v5:
time: 54.8 us; the launch traced here: 54.6 us
  Pallas kernels  53.9 us (98%)
  between operations  0.64 us (1%)
    pallas_call x1, Pallas kernels, whole(): pl.pallas_call(whole_kernel, name='whole', out_shape=(jax.ShapeDtypeStruc...  51.9 us
    pallas_call x1, Pallas kernels, hand_over(): pl.pallas_call(hand_over_kernel, name='hand_over', out_shape=tuple((jax.S...  1.99 us

profile of v5, /device:TPU:1, one launch (start us, length us, event | category | flops | bytes accessed | tf_op | source)
XLA Modules:
  0.0 54.6 jit_solution(12059584984329521579)
XLA Ops:
  0.6 51.9 %whole.1 = (bf16[192,1024]{1,0:T(8,128)(2,1)}, bf16[192,128]{1,0:T(8,128)(2,1)}, bf16[192,128]{1,0:T(8,128)(2,1)}, f32[16]{0:T(128)}) custom-call(bf16[192,1024]{1,0:T(8,128)(2,1)} %q_ref.1, bf16[192,1024]{1,0:T(8,128)(2,1)} %g_ref.1, bf16[192,128]{1,0:T(8,128)(2,1)} %k_hbm.1, bf16[192,128]{1,0:T(8,128)(2,1)} %v_hbm.1, s32[1,192]{1,0:T(1,128)} %bitcast.1, ...), custom_call_target="tpu_custom_call" | custom-call | tf_op jit(solution)/shard_map/whole/pallas_call | solution.py:494
  52.6 2.0 %hand_over.1 = (bf16[192,1024]{1,0:T(8,128)(2,1)}, bf16[192,128]{1,0:T(8,128)(2,1)}, bf16[192,128]{1,0:T(8,128)(2,1)}, f32[16]{0:T(128)}) custom-call(bf16[192,1024]{1,0:T(8,128)(2,1)} %get-tuple-element.8.refs_0_, bf16[192,128]{1,0:T(8,128)(2,1)} %get-tuple-element.9.refs_1_, bf16[192,128]{1,0:T(8,128)(2,1)} %get-tuple-element.10.refs_2_, ...), custom_call_target="tpu_custom_call" | custom-call | tf_op jit(solution)/shard_map/hand_over/pallas_call | solution.py:568

commit v6 on v5

--- a/solution.py
+++ b/solution.py
@@ -543,7 +543,7 @@
     moves = []
     for i in range(n):
         src, dst, via = refs[i], refs[n + i], refs[2 * n + i]
-        parts = [pl.ds(r, 48) for r in range(0, ROWS, 48)] if src.shape[1:] == (1024,) else [None]
+        parts = [pl.ds(r, 16) for r in range(0, ROWS, 16)] if src.shape[1:] == (1024,) else [None]
         for part in parts:
             ref = [r if part is None else r.at[part] for r in (src, via, dst)]
             k = len(moves)

time: 54.8 us -> 54.7 us (level)
  no operation moved by 1% of the time
where the time goes in v6:
time: 54.7 us; the launch traced here: 54.5 us
  Pallas kernels  53.9 us (99%)
  between operations  0.64 us (1%)
    pallas_call x1, Pallas kernels, whole(): pl.pallas_call(whole_kernel, name='whole', out_shape=(jax.ShapeDtypeStruc...  51.9 us
    pallas_call x1, Pallas kernels, hand_over(): pl.pallas_call(hand_over_kernel, name='hand_over', out_shape=tuple((jax.S...  1.93 us

profile of v6, /device:TPU:1, one launch (start us, length us, event | category | flops | bytes accessed | tf_op | source)
XLA Modules:
  0.0 54.5 jit_solution(5746454486465880839)
XLA Ops:
  0.6 51.9 %whole.1 = (bf16[192,1024]{1,0:T(8,128)(2,1)}, bf16[192,128]{1,0:T(8,128)(2,1)}, bf16[192,128]{1,0:T(8,128)(2,1)}, f32[16]{0:T(128)}) custom-call(bf16[192,1024]{1,0:T(8,128)(2,1)} %q_ref.1, bf16[192,1024]{1,0:T(8,128)(2,1)} %g_ref.1, bf16[192,128]{1,0:T(8,128)(2,1)} %k_hbm.1, bf16[192,128]{1,0:T(8,128)(2,1)} %v_hbm.1, s32[1,192]{1,0:T(1,128)} %bitcast.1, ...), custom_call_target="tpu_custom_call" | custom-call | tf_op jit(solution)/shard_map/whole/pallas_call | solution.py:494
  52.6 1.9 %hand_over.1 = (bf16[192,1024]{1,0:T(8,128)(2,1)}, bf16[192,128]{1,0:T(8,128)(2,1)}, bf16[192,128]{1,0:T(8,128)(2,1)}, f32[16]{0:T(128)}) custom-call(bf16[192,1024]{1,0:T(8,128)(2,1)} %get-tuple-element.8.refs_0_, bf16[192,128]{1,0:T(8,128)(2,1)} %get-tuple-element.9.refs_1_, bf16[192,128]{1,0:T(8,128)(2,1)} %get-tuple-element.10.refs_2_, ...), custom_call_target="tpu_custom_call" | custom-call | tf_op jit(solution)/shard_map/hand_over/pallas_call | solution.py:568
